TPU v7x, 512 devices: a whole 4x8x8 slice. The times are simulated.
512 devices in a mesh: pool: 128 (over z, y, core), mlp: 4 (over x).
Axes of the slice: x: 4, y: 8, z: 8, core: 2. Of those that a mesh axis runs over, the one named last changes fastest.
Arguments:
- residual_in: bfloat16 [256, 3072], P('pool', 'mlp'), may hold values from -6 to 6
- query_new: bfloat16 [256, 3072], P('pool', 'mlp'), may hold values from -6 to 6
- key_new: bfloat16 [256, 3072], P('pool', 'mlp'), may hold values from -6 to 6
- value_new: bfloat16 [256, 3072], P('pool', 'mlp'), may hold values from -6 to 6
- key_cache: bfloat16 [640, 256, 3072], P('pool', None, 'mlp'), may hold values from -240 to 240
- value_cache: bfloat16 [640, 256, 3072], P('pool', None, 'mlp'), may hold values from -6 to 6
- block_table: int32 [256, 8], P('pool'), may hold values from -1 to 639, as said below
- lengths: int32 [256], P('pool'), may hold values from 1 to 2048, as said below
- out_weight: bfloat16 [3072, 3072], P('mlp', 'pool'), may hold values from -0.109375 to 0.109375
- norm_gain: bfloat16 [3072], P('mlp'), may hold values from 0.25 to 1.75
- gate_weight: bfloat16 [3072, 8192], P('mlp', 'pool'), may hold values from -0.109375 to 0.109375
- up_weight: bfloat16 [3072, 8192], P('mlp', 'pool'), may hold values from -0.109375 to 0.109375
- down_weight: bfloat16 [8192, 3072], P('pool', 'mlp'), may hold values from -0.0625 to 0.0625
Outputs:
- layer_out: bfloat16 [256, 3072], P('pool', 'mlp')
Inputs may be any that keep to these rules, and one draw needn't show every extreme that they name: `block_table`: row r lists ceil(lengths[r] / 256) distinct block numbers followed by -1; no block is listed twice in the whole table. `lengths`: some request holds exactly 2048 tokens.
All inputs are finite; a program needn't handle non-finite values.
Results may differ from a plain program's by a relative error of at most 0.012.
Values may be sent and summed in bfloat16 or wider, within the bound.
A program may use at most 64 MiB of HBM per device.

v0:
```python
import math

import jax
import jax.numpy as jnp
from jax import lax
from jax.sharding import PartitionSpec as P

HD = 96


def rotate(values, positions):
    half_size = values.shape[-1] // 2
    inverse_freq = 10000.0 ** (-(2.0 * jnp.arange(half_size, dtype=jnp.float32)) / values.shape[-1])
    angles = positions.astype(jnp.float32)[:, None, None] * inverse_freq[None, None, :]
    cosine = jnp.cos(angles)
    sine_part = jnp.sin(angles)
    first = values[..., :half_size]
    second = values[..., half_size:]
    return jnp.concatenate(
        [first * cosine - second * sine_part, second * cosine + first * sine_part], -1
    )


def per_device(
    residual_in,
    query_new,
    key_new,
    value_new,
    key_cache,
    value_cache,
    block_table,
    lengths,
    out_weight,
    norm_gain,
    gate_weight,
    up_weight,
    down_weight,
):
    rows_dev, width_dev = residual_in.shape
    head_size = HD
    heads_dev = width_dev // head_size
    blocks_dev, block_len = (key_cache.shape[0], key_cache.shape[1])
    pool_index = lax.axis_index("pool")
    mlp_index = lax.axis_index("mlp")
    requests = rows_dev * lax.axis_size("pool")
    score_scale = 1.0 / math.sqrt(head_size)
    queries = rotate(
        query_new.astype(jnp.float32).reshape(rows_dev, heads_dev, head_size), lengths
    ).astype(jnp.bfloat16)
    new_keys = rotate(
        key_new.astype(jnp.float32).reshape(rows_dev, heads_dev, head_size), lengths
    ).astype(jnp.bfloat16)
    new_values = value_new.reshape(rows_dev, heads_dev, head_size)
    all_queries = lax.all_gather(queries.reshape(rows_dev, width_dev), "pool", axis=0, tiled=True)
    all_tables, all_lengths = (
        lax.all_gather(block_table, "pool", axis=0, tiled=True),
        lax.all_gather(lengths, "pool", axis=0, tiled=True),
    )
    held_ids = pool_index * blocks_dev + jnp.arange(blocks_dev, dtype=jnp.int32)
    matches = all_tables[None, :, :] == held_ids[:, None, None]
    holder = jnp.any(matches, 2)
    block_index = jnp.sum(
        jnp.where(matches, jnp.arange(all_tables.shape[1], dtype=jnp.int32)[None, None, :], 0),
        (1, 2),
    )
    valid_len = jnp.sum(jnp.where(holder, all_lengths[None, :], 0), 1)
    block_query = jnp.dot(
        holder.astype(jnp.bfloat16), all_queries, preferred_element_type=jnp.float32
    ).astype(jnp.bfloat16)
    block_query = block_query.reshape(blocks_dev, heads_dev, head_size)
    key_rows = key_cache.reshape(blocks_dev, block_len, heads_dev, head_size)
    value_rows = value_cache.reshape(blocks_dev, block_len, heads_dev, head_size)
    scores = (
        jnp.einsum("bhd,bthd->bht", block_query, key_rows, preferred_element_type=jnp.float32)
        * score_scale
    )
    token_pos = block_index[:, None] * block_len + jnp.arange(block_len, dtype=jnp.int32)[None, :]
    valid_mask = token_pos < valid_len[:, None]
    scores = jnp.where(valid_mask[:, None, :], scores, -1e30)
    block_max = jnp.max(scores, 2)
    self_score = (
        jnp.sum(queries.astype(jnp.float32) * new_keys.astype(jnp.float32), -1) * score_scale
    )
    request_max = jnp.max(jnp.where(holder[:, :, None], block_max[:, None, :], -1e30), 0)
    lowest = jnp.full((requests, heads_dev), -1e30, jnp.float32)
    own_scores = lax.dynamic_update_slice_in_dim(lowest, self_score, pool_index * rows_dev, 0)
    maxima_all = lax.pmax(jnp.maximum(request_max, own_scores), "pool")
    block_shift = jnp.sum(jnp.where(holder[:, :, None], maxima_all[None, :, :], 0.0), 1)
    weights = jnp.where(valid_mask[:, None, :], jnp.exp(scores - block_shift[:, :, None]), 0.0)
    block_totals = jnp.sum(weights, 2)
    block_numer = jnp.einsum(
        "bht,bthd->bhd",
        weights.astype(jnp.bfloat16),
        value_rows,
        preferred_element_type=jnp.float32,
    )
    block_numer = block_numer.reshape(blocks_dev, width_dev)
    holder_float = holder.astype(jnp.float32)
    numer_rows = jnp.einsum("br,bk->rk", holder_float, block_numer, precision=lax.Precision.HIGHEST)
    total_rows = jnp.einsum(
        "br,bh->rh", holder_float, block_totals, precision=lax.Precision.HIGHEST
    )
    numerator, totals = (
        lax.psum_scatter(numer_rows, "pool", scatter_dimension=0, tiled=True),
        lax.psum_scatter(total_rows, "pool", scatter_dimension=0, tiled=True),
    )
    own_max = lax.dynamic_slice_in_dim(maxima_all, pool_index * rows_dev, rows_dev, 0)
    numerator = numerator.reshape(rows_dev, heads_dev, head_size)
    self_weight = jnp.exp(self_score - own_max)
    totals = totals + self_weight
    self_low = lax.optimization_barrier(self_weight.astype(jnp.bfloat16))
    numerator = numerator + self_low.astype(jnp.float32)[:, :, None] * new_values.astype(
        jnp.float32
    )
    attended = (numerator / totals[:, :, None]).astype(jnp.bfloat16).reshape(rows_dev, width_dev)
    head_part = jnp.dot(
        lax.all_gather(attended, "pool", axis=0, tiled=True),
        out_weight,
        preferred_element_type=jnp.float32,
    )
    head_sum = lax.psum(head_part, "mlp").astype(jnp.bfloat16)
    head_out = lax.all_to_all(head_sum, "pool", split_axis=0, concat_axis=1, tiled=True)
    full_input, full_gain = (
        lax.all_gather(residual_in, "mlp", axis=1, tiled=True),
        lax.all_gather(norm_gain, "mlp", axis=0, tiled=True),
    )
    residual = full_input.astype(jnp.float32) + head_out.astype(jnp.float32)
    mean_square = jnp.mean(residual * residual, -1, keepdims=True)
    normed = (residual * lax.rsqrt(mean_square + 1e-05) * full_gain.astype(jnp.float32)).astype(
        jnp.bfloat16
    )
    own_normed = lax.dynamic_slice_in_dim(normed, mlp_index * width_dev, width_dev, 1)
    ff_dev = gate_weight.shape[1]
    portion = lax.all_gather(own_normed, "pool", axis=0, tiled=True)
    gate_up = jnp.concatenate(
        [
            jnp.dot(portion, gate_weight, preferred_element_type=jnp.float32),
            jnp.dot(portion, up_weight, preferred_element_type=jnp.float32),
        ],
        1,
    )
    summed = lax.psum(gate_up.astype(jnp.bfloat16), "mlp").astype(jnp.float32)
    hidden = (jax.nn.silu(summed[:, :ff_dev]) * summed[:, ff_dev:]).astype(jnp.bfloat16)
    down_out = lax.psum_scatter(
        jnp.dot(hidden, down_weight, preferred_element_type=jnp.float32),
        "pool",
        scatter_dimension=0,
        tiled=True,
    )
    own_residual = lax.dynamic_slice_in_dim(residual, mlp_index * width_dev, width_dev, 1)
    return (own_residual + down_out).astype(jnp.bfloat16)


def solution(mesh):
    in_specs = (
        P("pool", "mlp"),
        P("pool", "mlp"),
        P("pool", "mlp"),
        P("pool", "mlp"),
        P("pool", None, "mlp"),
        P("pool", None, "mlp"),
        P("pool", None),
        P("pool"),
        P("mlp", "pool"),
        P("mlp"),
        P("mlp", "pool"),
        P("mlp", "pool"),
        P("pool", "mlp"),
    )
    out_specs = P("pool", "mlp")
    return jax.shard_map(
        per_device, mesh=mesh, in_specs=in_specs, out_specs=out_specs, check_vma=False
    )
```

profile of v0, /device:TPU:1, one launch (start us, length us, event | category | flops | bytes accessed | tf_op | source)
XLA Modules:
  0.0 1296.5 jit_solution(4542194813107905304)
XLA Ops:
  6.6 58.5 %all-gather = s32[128,2,8]{2,1,0:T(2,128)S(1)} all-gather(s32[1,2,8]{2,1,0:T(2,128)} %bitcast.51), channel_id=1, replica_groups=mesh['pool'=128,'mlp'=4] {'pool'}, dimensions={0}, use_global_device_ids=true | all-gather | bytes 8256 | tf_op jit(solution)/shard_map/all_gather | solution.py:56
  66.2 0.8 reshape.161
  67.0 0.8 reshape.163
  68.3 48.8 %all-gather.1 = bf16[128,2,768]{2,1,0:T(2,128)(2,1)S(1)} all-gather(bf16[1,2,768]{2,1,0:T(2,128)(2,1)S(1)} %reshape.170), channel_id=1, replica_groups=mesh['pool'=128,'mlp'=4] {'pool'}, dimensions={0}, use_global_device_ids=true | all-gather | bytes 396288 | tf_op jit(solution)/shard_map/all_gather | solution.py:54
  117.5 2.7 copy.32
  120.2 0.7 fusion.20
  121.8 17.0 %all-reduce = s32[256]{0:T(256)S(1)} all-reduce(s32[256]{0:T(256)S(1)} %dynamic-update-slice), channel_id=1, replica_groups=mesh['pool'=128,'mlp'=4] {'pool'}, use_global_device_ids=true, to_apply=%add | all-reduce | flops 256 | bytes 2048
  139.9 255.5 %pmax.7 = f32[256,8]{0,1:T(8,128)S(1)} all-reduce(f32[256,8]{0,1:T(8,128)S(1)} %max.5), channel_id=1, replica_groups=mesh['pool'=128,'mlp'=4] {'pool'}, use_global_device_ids=true, to_apply=%region_6.7 | all-reduce | flops 2048 | bytes 16384 | tf_op jit(solution)/shard_map/pmax | solution.py:87
  395.7 2.7 copy.34
  399.1 1.4 fusion.22
  401.6 486.0 %all-reduce.2 = f32[256,8]{1,0:T(8,128)S(1)} all-reduce(f32[256,8]{1,0:T(8,128)S(1)} %fusion.23), channel_id=3, replica_groups=mesh['pool'=128,'mlp'=4] {'pool'}, use_global_device_ids=true, to_apply=%region_10.11.clone | all-reduce | flops 2048 | bytes 16384
  888.2 0.8 fusion.16
  889.0 51.6 %all-gather.2 = bf16[128,2,768]{2,1,0:T(2,128)(2,1)S(1)} all-gather(bf16[1,2,768]{2,1,0:T(2,128)(2,1)S(1)} %fusion.16), channel_id=1, replica_groups=mesh['pool'=128,'mlp'=4] {'pool'}, dimensions={0}, use_global_device_ids=true | all-gather | bytes 396288 | tf_op jit(solution)/shard_map/all_gather | solution.py:117
  941.0 13.3 %psum.14 = bf16[256,24]{0,1:T(8,128)(2,1)S(1)} all-reduce(f32[256,24]{0,1:T(8,128)S(1)} %fusion.24), channel_id=1, replica_groups=mesh['pool'=128,'mlp'=4] {'mlp'}, use_global_device_ids=true, to_apply=%region_11.12 | all-reduce | flops 6144 | bytes 36864 | tf_op jit(solution)/shard_map/psum | solution.py:121
  954.3 0.7 copy.38
  955.1 11.4 all-to-all-start
  966.5 9.0 all-gather.3
  975.6 8.9 all_gather.21
  984.9 57.5 %all-gather.4 = bf16[128,2,768]{2,1,0:T(2,128)(2,1)S(1)} all-gather(bf16[1,2,768]{2,1,0:T(2,128)(2,1)S(1)} %fusion.15), channel_id=1, replica_groups=mesh['pool'=128,'mlp'=4] {'pool'}, dimensions={0}, use_global_device_ids=true | all-gather | bytes 396288 | tf_op jit(solution)/shard_map/all_gather | solution.py:134
  1043.9 44.8 %all-reduce.8.cloned.1.call-done = bf16[256,128]{0,1:T(8,128)(2,1)} async-done(((bf16[256,128]{0,1:T(8,128)(2,1)}), bf16[256,128]{0,1:T(8,128)(2,1)}) %all-reduce.8.cloned.1.call-update) | async-done | bytes 65552 | tf_op jit(solution)/shard_map/psum | solution.py:142
  1088.6 0.8 convert_element_type.91
  1089.5 1.2 fusion.7
  1090.7 197.9 %all-reduce.12.cloned.1.call-done = f32[256,768]{1,0:T(8,128)} async-done(((f32[256,768]{1,0:T(8,128)}), f32[256,768]{1,0:T(8,128)}) %all-reduce.12.cloned.1.call-update) | async-done | bytes 786448
  1288.7 1.3 fusion.12
  (82 shorter events, 7.6 us)
Async XLA Ops:
  6.5 1083.0 %copy-start = (bf16[64,768]{1,0:T(8,128)(2,1)S(1)}, bf16[64,768]{1,0:T(8,128)(2,1)}, u32[]{:S(2)}) copy-start(bf16[64,768]{1,0:T(8,128)(2,1)} %param.25) | copy-start | bytes 294916
  6.5 881.7 %all-reduce.10.cloned.1.call-start = ((), (), s32[]{:S(2)}) async-start(), calls=%async_computation.2 | async-start | bytes 1572864
  117.5 2.7 copy-start.7
  117.5 4.1 copy-start.8
  398.4 489.8 %copy-start.4 = (bf16[2,768]{1,0:T(2,128)(2,1)S(1)}, bf16[2,768]{1,0:T(2,128)(2,1)}, u32[]{:S(2)}) copy-start(bf16[2,768]{1,0:T(2,128)(2,1)} %param.16) | copy-start | bytes 9220
  399.0 541.8 %copy-start.3 = (bf16[768,24]{0,1:T(8,128)(2,1)S(1)}, bf16[768,24]{0,1:T(8,128)(2,1)}, u32[]{:S(2)}) copy-start(bf16[768,24]{0,1:T(8,128)(2,1)} %param.21) | copy-start | bytes 110596
  399.1 567.4 %copy-start.6 = (bf16[768]{0:T(1024)(128)(2,1)S(1)}, bf16[768]{0:T(1024)(128)(2,1)}, u32[]{:S(2)}) copy-start(bf16[768]{0:T(1024)(128)(2,1)} %param.22) | copy-start | bytes 4612
  399.1 576.4 %copy-start.5 = (bf16[2,768]{1,0:T(2,128)(2,1)S(1)}, bf16[2,768]{1,0:T(2,128)(2,1)}, u32[]{:S(2)}) copy-start(bf16[2,768]{1,0:T(2,128)(2,1)} %param.13) | copy-start | bytes 9220
  887.7 154.9 %copy-start.1 = (bf16[768,64]{0,1:T(8,128)(2,1)S(1)}, bf16[768,64]{0,1:T(8,128)(2,1)}, u32[]{:S(2)}) copy-start(bf16[768,64]{0,1:T(8,128)(2,1)} %param.24) | copy-start | bytes 294916
  940.6 102.2 %copy-start.2 = (bf16[768,64]{0,1:T(8,128)(2,1)S(1)}, bf16[768,64]{0,1:T(8,128)(2,1)}, u32[]{:S(2)}) copy-start(bf16[768,64]{0,1:T(8,128)(2,1)} %param.23) | copy-start | bytes 294916
  955.1 29.5 %all-to-all-start = ((bf16[128,2,24]{2,1,0:T(2,128)(2,1)}), bf16[128,2,24]{2,1,0:T(2,128)(2,1)S(1)}, u32[]{:S(2)}, u32[]{:S(2)}) async-start(bf16[128,2,24]{2,1,0:T(2,128)(2,1)} %bitcast.10), calls=%async_computation | async-start | bytes 131072 | tf_op jit(solution)/shard_map/all_to_all | solution.py:122
  966.4 122.2 %all-reduce.8.cloned.1.call-start = ((), (), s32[]{:S(2)}) async-start(), calls=%async_computation.1 | async-start | bytes 131072 | tf_op jit(solution)/shard_map/psum | solution.py:142
  1043.8 244.9 %all-reduce.12.cloned.1.call-start = ((), (), s32[]{:S(2)}) async-start(), calls=%async_computation.3 | async-start | bytes 1572864
Sparse Core Ops, SparseCore 0:
  400.7 185.9 all-reduce.9
  1043.9 44.6 all-reduce.7
  1092.2 196.4 all-reduce.11
where the time goes:
time: 1300 us
  blocking collectives  1010 us (78%)
  waiting for transfers between devices  243 us (19%)
  between operations  14.8 us (1%)
    unnamed x2, blocking collectives  503 us
    pmax x1, blocking collectives, per_device(): maxima_all = lax.pmax(jnp.maximum(request_max, own_scores), 'pool')  256 us
    unnamed x5, waiting for transfers between devices  198 us
    all_gather x1, blocking collectives, per_device(): lax.all_gather(block_table, 'pool', axis=0, tiled=True)  58.5 us
    all_gather x1, blocking collectives, per_device(): portion = lax.all_gather(own_normed, 'pool', axis=0, tiled=True)  57.5 us
    all_gather x1, blocking collectives, per_device(): lax.all_gather(attended, 'pool', axis=0, tiled=True)  51.6 us
    all_gather x1, blocking collectives, per_device(): lax.all_gather(queries.reshape(rows_dev, width_dev), 'pool', axis=0, tile...  48.8 us
    psum x1, waiting for transfers between devices, per_device(): summed = lax.psum(gate_up.astype(jnp.bfloat16), 'mlp').astype(jnp.float32)  44.8 us
  transfers between devices with their start and end apart: 4, of which 2 were waited for; matrix products, arithmetic and copies ran while one was open for 0% of the time, Pallas kernels for 0%

commit v1 on v0

v1 whole, which is shorter than its diff:
```python
import math

import jax
import jax.numpy as jnp
import numpy as np
from jax import lax
from jax.experimental import pallas as pl
from jax.experimental.pallas import tpu as pltpu
from jax.sharding import PartitionSpec as P

HD = 96
N = 8
X = 4
REQ = 256
DEV = 768
HALF = 384
BLK = 5
BT = 256
FFD = 64
MESH = pl.DeviceIdType.MESH
F32 = jnp.float32
BF16 = jnp.bfloat16


def tables():
    lane = np.arange(1024)
    s, r = lane // 128, lane % 128
    f, core, b = r // 10, (r // 5) % 2, r % 5
    ids = np.stack([((f * 16 + s * 2 + core) * 5 + b), ((s * 16 + f * 2 + core) * 5 + b)])
    ids = np.where(r[None] < 80, ids, -7).astype(np.float32)
    k = np.arange(768)
    s, f, core, i = k // 96, (k // 12) % 8, (k // 6) % 2, k % 6
    feats = []
    for z, y in ((f, s), (s, f)):
        feats.append(384 * (z % 2) + 48 * y + 24 * core + 6 * (z // 2) + i)
    feats = np.stack(feats).astype(np.float32)
    return ids, feats


def rotate(values, positions):
    half_size = values.shape[-1] // 2
    inverse_freq = 10000.0 ** (-(2.0 * jnp.arange(half_size, dtype=F32)) / values.shape[-1])
    angles = positions.astype(F32)[:, None, None] * inverse_freq[None, None, :]
    cosine = jnp.cos(angles)
    sine_part = jnp.sin(angles)
    first = values[..., :half_size]
    second = values[..., half_size:]
    return jnp.concatenate(
        [first * cosine - second * sine_part, second * cosine + first * sine_part], -1
    )


def nt(a, b):
    return lax.dot_general(a, b, (((1,), (1,)), ((), ())), preferred_element_type=F32)


def nn(a, b):
    return jnp.dot(a, b, preferred_element_type=F32)


def iota(shape, dim):
    return lax.broadcasted_iota(jnp.int32, shape, dim)


class Net:
    def __init__(self, send, recv):
        self.p = lax.axis_index("pool")
        self.x = lax.axis_index("mlp")
        self.c = self.p % 2
        self.y = (self.p // 2) % N
        self.z = self.p // (2 * N)
        c = self.c
        self.fi = self.z * (1 - c) + self.y * c
        self.si = self.y * (1 - c) + self.z * c
        self.sib = self.p + 1 - 2 * c
        self.send, self.recv = send, recv
        self.ns = self.nr = 0
        self.sent = []

    def recvs(self, count):
        base = self.nr
        self.nr += count
        return base

    def chip(self, z, y, core):
        return z * (2 * N) + y * 2 + core

    def put(self, src, dst, recv_index, pool, mlp=None):
        copy = pltpu.make_async_remote_copy(
            src_ref=src,
            dst_ref=dst,
            send_sem=self.send.at[self.ns],
            recv_sem=self.recv.at[recv_index],
            device_id=(pool, self.x if mlp is None else mlp),
            device_id_type=MESH,
        )
        self.ns += 1
        copy.start()
        self.sent.append(copy)
        return copy

    def got(self, dst, recv_index):
        pltpu.make_async_remote_copy(
            src_ref=dst,
            dst_ref=dst,
            send_sem=self.send.at[0],
            recv_sem=self.recv.at[recv_index],
            device_id=(self.sib, self.x),
            device_id_type=MESH,
        ).wait_recv()

    def spread(self, src, slots, base, along_first=True, pick=False):
        z, y, c = self.z, self.y, self.c
        own_index = self.fi if along_first else self.si
        for k in range(1, N):
            for d in (0, 1):
                on_z = (d == 0) == along_first
                me = z if on_z else y
                t = (me + k) % N
                pool = self.chip(t, y, d) if on_z else self.chip(z, t, d)
                slot = me * 2 + c
                self.put(
                    src.at[d, t] if pick else src.at[d], slots.at[slot], base + slot, pool
                )
        sib_index = self.si if along_first else self.fi
        slot = sib_index * 2 + c
        self.put(
            src.at[1 - c, sib_index] if pick else src.at[1 - c],
            slots.at[slot],
            base + slot,
            self.sib,
        )
        slots[own_index * 2 + c] = src[c, own_index] if pick else src[c]

    def spread_wait(self, slots, base, own_index):
        own = own_index * 2 + self.c
        for k in range(1, 2 * N):
            slot = (own + k) % (2 * N)
            self.got(slots.at[slot], base + slot)

    def line_send(self, bufs, bases):
        c, si = self.c, self.si
        for k in range(1, N):
            t = (si + k) % N
            pool = self.fi * (16 - 14 * c) + t * (2 + 14 * c) + c
            for view, (b, _) in zip(bufs, bases):
                self.put(view(c, si), view(c, si), b + si, pool)
        for view, (_, b) in zip(bufs, bases):
            self.put(view(c, si), view(c, si), b + si, self.sib)

    def line_forward(self, bufs, bases):
        c, si = self.c, self.si
        for k in range(1, N):
            s = (si + N - k) % N
            for view, (b, b2) in zip(bufs, bases):
                self.got(view(c, s), b + s)
                self.put(view(c, s), view(c, s), b2 + s, self.sib)

    def line_wait(self, bufs, bases):
        c = self.c
        for s in range(N):
            for view, (_, b2) in zip(bufs, bases):
                self.got(view(1 - c, s), b2 + s)


def kernel(
    pay_ref, vr_ref, ids_ref, feat_ref, wo_ref, gain_ref, gate_ref, up_ref, down_ref,
    key_hbm, val_hbm, out_ref,
    kbuf, vbuf, slot1, slot2, line1, line2, g1, gv, gr,
    acc_src, lse_src, acc_slot, lse_slot, acc_line, ga, gl,
    bias, ebuf, attb, wgp, s3_src, s3_slot, h_src, h_slot, h_line, gh,
    gu_buf, sq_buf, dbuf, d_slot, b_src, b_slot,
    send, recv, local,
):
    net = Net(send, recv)
    p, x, c, y, z, fi, si = net.p, net.x, net.c, net.y, net.z, net.fi, net.si
    group = p // 32
    rest = p % 32

    kcopy = pltpu.make_async_copy(key_hbm, kbuf, local.at[0])
    vcopy = pltpu.make_async_copy(val_hbm, vbuf, local.at[1])
    kcopy.start()
    vcopy.start()

    barrier = pltpu.get_barrier_semaphore()

    def hello(pool, mlp):
        pl.semaphore_signal(barrier, inc=1, device_id=(pool, mlp), device_id_type=MESH)

    for k in range(1, N):
        for e in (0, 1):
            hello(net.chip((z + k) % N, y, e), x)
            hello(net.chip(z, (y + k) % N, e), x)
    hello(net.sib, x)
    for k in range(1, X):
        hello(p, (x + k) % X)
    home = group == x
    for k in range(X):

        @pl.when(jnp.logical_not(jnp.logical_and(home, x == k)))
        def _():
            hello(32 * x + rest, k)

    pl.semaphore_wait(barrier, 36 - jnp.where(home, 1, 0))

    r_pay, r_vr = net.recvs(16), net.recvs(16)
    net.spread(pay_ref, slot1, r_pay)
    net.spread(vr_ref, slot2, r_vr)

    q_view = lambda d, s: g1.at[d, s]
    v_view = lambda d, s: gv.at[d, s]
    r_view = lambda d, s: gr.at[d, s]
    q_base = [(net.recvs(N), net.recvs(N))]
    v_base = [(net.recvs(N), net.recvs(N))]
    r_base = [(net.recvs(N), net.recvs(N))]

    net.spread_wait(slot1, r_pay, fi)
    for j in range(16):
        line1[2 * j : 2 * j + 2, :] = slot1[j]
    g1[c, si] = line1[...].astype(BF16)
    net.line_send([q_view], q_base)
    net.spread_wait(slot2, r_vr, fi)
    for j in range(16):
        line2[2 * j : 2 * j + 2, :] = slot2[j]
    gv[c, si] = line2[:, :HALF].astype(BF16)
    gr[c, si] = line2[:, HALF:].astype(BF16)
    net.line_send([v_view], v_base)

    gain = gain_ref[...].astype(F32)
    wg = jnp.concatenate([gate_ref[...].astype(F32).T, up_ref[...].astype(F32).T], 0)
    wg = (wg * gain).astype(BF16)
    for d in (0, 1):
        feat = feat_ref[d : d + 1, :]
        for g in range(6):
            cols = feat[:, 128 * g : 128 * g + 128]
            place = (iota((DEV, 128), 0).astype(F32) == cols).astype(F32).astype(BF16)
            wgp[d, :, 128 * g : 128 * g + 128] = nn(wg, place).astype(BF16)
    wot = wo_ref[...].astype(F32).T.astype(BF16)
    o_row, n_col = iota((REQ, REQ), 0), iota((REQ, REQ), 1)
    nat_row = ((o_row >> 2) & 7) * 32 + (o_row >> 5) * 4 + (o_row & 3)
    nat_col = ((n_col >> 2) & 7) * 32 + (n_col >> 5) * 4 + (n_col & 3)
    to_order0 = (nat_row == n_col).astype(F32).astype(BF16)
    to_natural = (o_row == nat_col).astype(F32).astype(BF16)

    net.line_forward([q_view], q_base)
    net.line_wait([q_view], q_base)

    metas = []
    queries = []
    own_len = None
    sub8 = iota((8, REQ), 0)
    for d in (0, 1):
        meta = g1[d, :, :, HALF:].reshape(REQ, 128).astype(F32)
        metas.append(meta)
        meta_t = meta.T
        tab = 16.0 * meta_t[0:16] + meta_t[16:32]
        onehot = jnp.zeros((8, REQ), F32)
        lens = []
        for b in range(BLK):
            match = (tab[0:8] == (p * BLK + b).astype(F32)).astype(F32)
            row = jnp.max(match, 0, keepdims=True)
            onehot = jnp.where(sub8 == b, row, onehot)
            left = match * (tab[8:9] - 256.0 * sub8.astype(F32))
            lens.append(jnp.sum(jnp.sum(left, 0, keepdims=True), 1, keepdims=True))
        own_len = lens
        queries.append(nn(onehot.astype(BF16), g1[d, :, :, :HALF].reshape(REQ, HALF)))
    lane = iota((8, DEV), 1)
    sub = iota((8, DEV), 0)
    head_mask = jnp.logical_and(lane >= 96 * sub, lane < 96 * sub + 96)
    query = jnp.concatenate(queries, 1)
    kcopy.wait()
    vcopy.wait()
    acc = jnp.zeros((8, DEV), F32)
    lane128 = iota((8, 128), 1)
    tiles = [jnp.zeros((8, 128), F32), jnp.zeros((8, 128), F32)]
    scale = 1.0 / math.sqrt(HD)
    for b in range(BLK):
        wide = jnp.where(head_mask, query[b : b + 1, :], 0.0).astype(BF16)
        scores = nt(wide, kbuf[b]) * scale
        valid = iota((8, BT), 1).astype(F32) < own_len[b]
        scores = jnp.where(valid, scores, -1e30)
        top = jnp.max(scores, 1, keepdims=True)
        weights = jnp.where(valid, jnp.exp(scores - top), 0.0)
        total = jnp.maximum(jnp.sum(weights, 1, keepdims=True), 1.0)
        numer = nn(weights.astype(BF16), vbuf[b]) / total
        row = jnp.sum(jnp.where(head_mask, numer, 0.0), 0, keepdims=True)
        acc = jnp.where(sub == b, row, acc)
        lse = top + jnp.log(total)
        for d, f in ((0, z), (1, y)):
            tiles[d] = jnp.where(lane128 == 10 * f + 5 * c + b, lse, tiles[d])
    for d in (0, 1):
        acc_src[d] = acc[:, HALF * d : HALF * d + HALF].astype(BF16)
        lse_src[d] = tiles[d]

    r_acc, r_lse = net.recvs(16), net.recvs(16)
    net.spread(acc_src, acc_slot, r_acc)
    net.spread(lse_src, lse_slot, r_lse)
    net.line_forward([v_view], v_base)
    for d in (0, 1):
        for s in range(N):
            ga[d, s, 80:128, :] = jnp.zeros((48, HALF), BF16)
    net.spread_wait(acc_slot, r_acc, fi)
    for j in range(16):
        acc_line[5 * j : 5 * j + 5, :] = acc_slot[j].astype(F32)[0:5]
    ga[c, si, 0:80, :] = acc_line[...].astype(BF16)
    net.spread_wait(lse_slot, r_lse, fi)
    line = lse_slot[0]
    for j in range(1, 16):
        line = line + lse_slot[j]
    gl[c, si] = line
    a_views = [lambda d, s: ga.at[d, s, pl.ds(0, 80)], lambda d, s: gl.at[d, s]]
    a_base = [(net.recvs(N), net.recvs(N)), (net.recvs(N), net.recvs(N))]
    net.line_send(a_views, a_base)
    net.line_send([r_view], r_base)

    for d in (0, 1):
        meta = metas[d]
        cols = [16.0 * meta[:, j : j + 1] + meta[:, 16 + j : 17 + j] for j in range(8)]
        for s in range(N):
            ids = ids_ref[d : d + 1, 128 * s : 128 * s + 128]
            hit = cols[0] == ids
            for j in range(1, 8):
                hit = jnp.logical_or(hit, cols[j] == ids)
            bias[d, :, 128 * s : 128 * s + 128] = jnp.where(hit, 0.0, -1e30)

    net.line_wait([v_view], v_base)
    net.line_forward(a_views, a_base)
    net.line_wait(a_views, a_base)

    for d in (0, 1):
        meta = metas[d]
        selfs, totals = [], []
        for h in range(4):
            own = meta[:, 32 + h : 33 + h] + meta[:, 36 + h : 37 + h] + meta[:, 40 + h : 41 + h]
            row = 4 * d + h
            score = jnp.concatenate([gl[d, s, row : row + 1, :] for s in range(N)], 1)
            logits = score + bias[d]
            top = jnp.maximum(jnp.max(logits, 1, keepdims=True), own)
            weights = jnp.exp(logits - top)
            own_weight = jnp.exp(own - top)
            totals.append(jnp.sum(weights, 1, keepdims=True) + own_weight)
            selfs.append(own_weight.astype(BF16).astype(F32))
            ebuf[h] = weights.astype(BF16)
        lane_r = iota((REQ, 128), 1)
        for g in range(3):
            block = ga[d, :, :, 128 * g : 128 * g + 128].reshape(1024, 128)
            low = lane_r < 96 - 32 * g
            numer = jnp.where(low, nn(ebuf[g], block), nn(ebuf[g + 1], block))
            value = gv[d, :, :, 128 * g : 128 * g + 128].reshape(REQ, 128).astype(F32)
            numer = numer + jnp.where(low, selfs[g], selfs[g + 1]) * value
            attb[d, :, 128 * g : 128 * g + 128] = (
                numer / jnp.where(low, totals[g], totals[g + 1])
            ).astype(BF16)
    att0 = nn(to_natural, attb[0]).astype(BF16)
    head = nt(wot[:, :HALF], att0) + nt(wot[:, HALF:], attb[1])

    r_s3 = net.recvs(X)
    for k in range(X):
        s3_src[k] = head[6 * k : 6 * k + 6]
    copies = []
    for k in range(X):
        is_self = jnp.logical_and(home, x == k)
        copies.append(
            pltpu.make_async_remote_copy(
                src_ref=s3_src.at[k],
                dst_ref=s3_slot.at[x],
                send_sem=send.at[net.ns + k],
                recv_sem=recv.at[r_s3 + x],
                device_id=(32 * k + rest, group),
                device_id_type=MESH,
            )
        )

        @pl.when(jnp.logical_not(is_self))
        def _(k=k):
            copies[k].start()

    @pl.when(home)
    def _():
        s3_slot[x] = s3_src[x]

    s3_sends = copies
    net.ns += X
    net.line_forward([r_view], r_base)
    net.line_wait([r_view], r_base)
    feature = 24 * rest + 6 * group + iota((8, HALF), 0)
    inputs = []
    for d in (0, 1):
        pick = jnp.logical_and(
            iota((8, HALF), 1) + HALF * d == feature, iota((8, HALF), 0) < 6
        )
        inputs.append(nt(pick.astype(F32).astype(BF16), gr[d].reshape(REQ, HALF)))
    piece = nt(inputs[0].astype(BF16), to_natural) + inputs[1]
    for k in range(X):

        @pl.when(jnp.logical_not(jnp.logical_and(home, x == k)))
        def _(k=k):
            net.got(s3_slot.at[k], r_s3 + k)

    total = (s3_slot[0] + s3_slot[1]) + (s3_slot[2] + s3_slot[3])
    piece = piece[0:6] + total.astype(BF16).astype(F32)
    h_src[0] = piece[:, :128]
    h_src[1] = piece[:, 128:]

    r_h = net.recvs(16)
    h_base = [(net.recvs(N), net.recvs(N))]
    h_view = lambda d, s: gh.at[d, s]
    net.spread(h_src, h_slot, r_h)
    net.spread_wait(h_slot, r_h, fi)
    for j in range(16):
        h_line[6 * j : 6 * j + 6, :] = h_slot[j]
    gh[c, si] = h_line[...].astype(BF16)
    net.line_send([h_view], h_base)
    net.line_forward([h_view], h_base)
    net.line_wait([h_view], h_base)

    for d in (0, 1):
        resid = gh[d].reshape(DEV, 128)
        gu_buf[x, :, 128 * d : 128 * d + 128] = nn(wgp[d], resid).astype(BF16)
        wide = resid.astype(F32)
        square = jnp.sum(wide * wide, 0, keepdims=True)
        sq_buf[x, :, 128 * d : 128 * d + 128] = jnp.broadcast_to(square, (8, 128))
    r_gu, r_sq = net.recvs(X), net.recvs(X)
    for k in range(1, X):
        net.put(gu_buf.at[x], gu_buf.at[x], r_gu + x, p, (x + k) % X)
        net.put(sq_buf.at[x], sq_buf.at[x], r_sq + x, p, (x + k) % X)
    own_resid = jnp.zeros((8, DEV), F32)
    for d in (0, 1):
        pick = iota((8, 128), 1) + 128 * d == 2 * p + iota((8, 128), 0)
        pick = jnp.logical_and(pick, iota((8, 128), 0) < 2)
        mine = nt(pick.astype(F32).astype(BF16), gh[d].reshape(DEV, 128)).astype(BF16)
        feat = feat_ref[d : d + 1, :]
        parts = []
        for g in range(6):
            place = iota((128, DEV), 0).astype(F32) + 128.0 * g == feat
            parts.append(nt(mine, place.astype(F32).astype(BF16)))
        own_resid = own_resid + jnp.concatenate(parts, 1)
    for k in range(1, X):
        t = (x + k) % X
        net.got(gu_buf.at[t], r_gu + t)
        net.got(sq_buf.at[t], r_sq + t)
    gu = gu_buf[0].astype(F32)
    square = sq_buf[0]
    for k in range(1, X):
        gu = gu + gu_buf[k].astype(F32)
        square = square + sq_buf[k]
    inv = lax.rsqrt(square[0:1] * (1.0 / (X * DEV)) + 1e-05)
    gate = gu[:FFD] * inv
    up = gu[FFD:] * inv
    hidden = gate / (1.0 + jnp.exp(-gate)) * up
    hidden_t = hidden.T.astype(BF16)

    down = down_ref[...]
    rows = [nn(to_order0, hidden_t).astype(BF16), hidden_t]
    for d in (0, 1):
        part = nn(rows[d], down[:, HALF * d : HALF * d + HALF]).astype(BF16)
        for s in range(N):
            dbuf[d, s] = part[32 * s : 32 * s + 32]
    r_d = net.recvs(16)
    net.spread(dbuf, d_slot, r_d, along_first=False, pick=True)
    net.spread_wait(d_slot, r_d, si)
    part = d_slot[0].astype(F32)
    for j in range(1, 16):
        part = part + d_slot[j].astype(F32)
    for f in range(N):
        for e in (0, 1):
            b_src[f, e] = part[4 * f + 2 * e : 4 * f + 2 * e + 2]
    r_b = net.recvs(16)
    own = c * N + fi
    for k in range(1, N):
        t = (fi + k) % N
        for e in (0, 1):
            pool = net.chip(t * (1 - c) + z * c, y * (1 - c) + t * c, e)
            net.put(b_src.at[t, e], b_slot.at[own], r_b + own, pool)
    net.put(b_src.at[fi, 1 - c], b_slot.at[own], r_b + own, net.sib)
    b_slot[own] = b_src[fi, c]
    for k in range(1, 16):
        slot = (own + k) % 16
        net.got(b_slot.at[slot], r_b + slot)
    for d in (0, 1):
        total = b_slot[N * d]
        for f in range(1, N):
            total = total + b_slot[N * d + f]
        out_ref[:, HALF * d : HALF * d + HALF] = (
            own_resid[0:2, HALF * d : HALF * d + HALF] + total
        ).astype(BF16)

    for copy in net.sent:
        copy.wait_send()
    for k in range(X):

        @pl.when(jnp.logical_not(jnp.logical_and(home, x == k)))
        def _(k=k):
            s3_sends[k].wait_send()


SENDS = 420
RECVS = 360


def scratch():
    v = pltpu.VMEM
    return [
        v((BLK, BT, DEV), BF16), v((BLK, BT, DEV), BF16),
        v((16, 2, 512), F32), v((16, 2, DEV), F32), v((32, 512), F32), v((32, DEV), F32),
        v((2, N, 32, 512), BF16), v((2, N, 32, HALF), BF16), v((2, N, 32, HALF), BF16),
        v((2, 8, HALF), BF16), v((2, 8, 128), F32), v((16, 8, HALF), BF16), v((16, 8, 128), F32),
        v((80, HALF), F32), v((2, N, 128, HALF), BF16), v((2, N, 8, 128), F32),
        v((2, REQ, 1024), F32), v((4, REQ, 1024), BF16), v((2, REQ, HALF), BF16),
        v((2, 128, DEV), BF16),
        v((X, 6, REQ), F32), v((X, 6, REQ), F32),
        v((2, 6, 128), F32), v((16, 6, 128), F32), v((96, 128), F32), v((2, N, 96, 128), BF16),
        v((X, 128, REQ), BF16), v((X, 8, REQ), F32),
        v((2, N, 32, HALF), BF16), v((16, 32, HALF), BF16), v((N, 2, 2, HALF), F32), v((16, 2, HALF), F32),
        pltpu.SemaphoreType.DMA((SENDS,)), pltpu.SemaphoreType.DMA((RECVS,)),
        pltpu.SemaphoreType.DMA((2,)),
    ]


def per_device(
    residual_in, query_new, key_new, value_new, key_cache, value_cache, block_table, lengths,
    out_weight, norm_gain, gate_weight, up_weight, down_weight,
):
    heads = DEV // HD
    queries = rotate(query_new.astype(F32).reshape(2, heads, HD), lengths).astype(BF16)
    new_keys = rotate(key_new.astype(F32).reshape(2, heads, HD), lengths).astype(BF16)
    queries = queries.astype(F32)
    self_score = jnp.sum(queries * new_keys.astype(F32), -1) * (1.0 / math.sqrt(HD))
    whole = jnp.concatenate([block_table, lengths[:, None]], 1)
    pad = jnp.zeros((2, 7), F32)
    high = (whole >> 4).astype(F32)
    low = (whole & 15).astype(F32)
    s1 = lax.reduce_precision(self_score, 8, 7)
    s2 = lax.reduce_precision(self_score - s1, 8, 7)
    s3 = lax.reduce_precision(self_score - s1 - s2, 8, 7)
    rest = jnp.zeros((2, 84), F32)
    flat = queries.reshape(2, DEV)
    pay = jnp.stack(
        [
            jnp.concatenate(
                [flat[:, HALF * d : HALF * d + HALF], high, pad, low, pad]
                + [s[:, 4 * d : 4 * d + 4] for s in (s1, s2, s3)]
                + [rest],
                1,
            )
            for d in (0, 1)
        ]
    )
    vr = jnp.stack(
        [
            jnp.concatenate(
                [a[:, HALF * d : HALF * d + HALF] for a in (value_new, residual_in)], 1
            ).astype(F32)
            for d in (0, 1)
        ]
    )
    ids, feats = tables()
    vm = pl.BlockSpec(memory_space=pltpu.VMEM)
    hbm = pl.BlockSpec(memory_space=pl.ANY)
    return pl.pallas_call(
        kernel,
        out_shape=jax.ShapeDtypeStruct((2, DEV), BF16),
        in_specs=[vm] * 9 + [hbm] * 2,
        out_specs=vm,
        scratch_shapes=scratch(),
        compiler_params=pltpu.CompilerParams(
            collective_id=0, has_side_effects=True, vmem_limit_bytes=48 * 1024 * 1024
        ),
        name="layer",
    )(
        pay, vr, jnp.asarray(ids), jnp.asarray(feats), out_weight, norm_gain.reshape(1, DEV),
        gate_weight, up_weight, down_weight, key_cache, value_cache,
    )


def solution(mesh):
    in_specs = (
        P("pool", "mlp"),
        P("pool", "mlp"),
        P("pool", "mlp"),
        P("pool", "mlp"),
        P("pool", None, "mlp"),
        P("pool", None, "mlp"),
        P("pool", None),
        P("pool"),
        P("mlp", "pool"),
        P("mlp"),
        P("mlp", "pool"),
        P("mlp", "pool"),
        P("pool", "mlp"),
    )
    out_specs = P("pool", "mlp")
    return jax.shard_map(
        per_device, mesh=mesh, in_specs=in_specs, out_specs=out_specs, check_vma=False
    )
```

time: 1300 us -> 112 us (0.09)
  blocking collectives: 1010 us -> 0 us
  waiting for transfers between devices: 243 us -> 0 us
  Pallas kernels: 0 us -> 96.6 us
  between operations: 14.8 us -> 0.07 us
    unnamed x2 -> x0, blocking collectives: 503 us -> none
    pmax x1 -> x0, blocking collectives: 256 us -> none  [per_device(): maxima_all = lax.pmax(jnp.maximum(request_max, own_scores), 'pool')]
    all_gather x6 -> x0, blocking collectives: 234 us -> none  [the longest x1 58.5 us: per_device(): lax.all_gather(block_table, 'pool', axis=0, tiled=True)]
    unnamed x5 -> x0, waiting for transfers between devices: 198 us -> none
    pallas_call x0 -> x1, Pallas kernels: none -> 96.6 us  [per_device(): pl.pallas_call(kernel, out_shape=jax.ShapeDtypeStruct((2, DEV), BF16), in...]
    psum x1 -> x0, waiting for transfers between devices: 44.8 us -> none  [per_device(): summed = lax.psum(gate_up.astype(jnp.bfloat16), 'mlp').astype(jnp.float32)]
    psum x1 -> x0, blocking collectives: 13.3 us -> none  [per_device(): head_sum = lax.psum(head_part, 'mlp').astype(jnp.bfloat16)]
  transfers between devices with their start and end apart: 4 -> 0, of which waited for: 2 -> 0; matrix products, arithmetic and copies ran while one was open for 0% -> 0% of each run, Pallas kernels for 0% -> 0%
where the time goes in v1:
time: 112 us
  Pallas kernels  96.6 us (86%)
  local copies, waits for them, and re-layouts  13.1 us (12%)
  other arithmetic  1.88 us (2%)
    pallas_call x1, Pallas kernels, per_device(): pl.pallas_call(kernel, out_shape=jax.ShapeDtypeStruct((2, DEV), BF16), in...  96.6 us
    unnamed x14, local copies, waits for them, and re-layouts  9 us

profile of v1, /device:TPU:1, one launch (start us, length us, event | category | flops | bytes accessed | tf_op | source)
XLA Modules:
  0.0 111.6 jit_solution(5111119970302296178)
XLA Ops:
  0.0 0.7 convert_element_type.46
  0.7 0.7 copy.16
  1.4 0.8 and_convert_fusion
  2.2 0.1 multiply_cosine_fusion
  2.3 0.7 reshape.143.gain_ref
  3.0 0.7 slice_bitcast_fusion.2
  3.7 0.8 reshape.145
  4.5 0.1 multiply_subtract_fusion
  4.6 0.8 reshape.148
  5.3 0.1 subtract_convert_fusion
  5.4 0.2 multiply_reduce_fusion
  5.6 0.1 fusion.4
  5.8 0.1 concatenate.47
  5.9 0.1 concatenate.48
  6.0 0.9 copy.17.wo_ref
  7.0 1.1 copy.18.gate_ref
  8.0 1.1 copy.19.up_ref
  9.1 1.5 %copy-done = bf16[5,256,768]{2,1,0:T(8,128)(2,1)S(1)} copy-done((bf16[5,256,768]{2,1,0:T(8,128)(2,1)S(1)}, bf16[5,256,768]{2,1,0:T(8,128)(2,1)}, u32[]{:S(2)}) %copy-start) | copy-done | bytes 1966104
  10.7 1.5 %copy-done.1 = bf16[5,256,768]{2,1,0:T(8,128)(2,1)S(1)} copy-done((bf16[5,256,768]{2,1,0:T(8,128)(2,1)S(1)}, bf16[5,256,768]{2,1,0:T(8,128)(2,1)}, u32[]{:S(2)}) %copy-start.1) | copy-done | bytes 1966104
  12.2 0.9 copy-done.2
  13.1 0.7 copy-done.3
  13.8 0.7 copy-done.4
  14.5 96.6 %layer.1 = bf16[2,768]{1,0:T(2,128)(2,1)S(1)} custom-call(f32[2,2,512]{2,1,0:T(2,128)S(1)} %pad_maximum_fusion.pay_ref, f32[2,2,768]{2,1,0:T(2,128)S(1)} %maximum_convert_fusion.1.vr_ref, f32[2,1024]{1,0:T(2,128)S(1)} %copy-done.3, f32[2,768]{1,0:T(2,128)S(1)} %copy-done.4, bf16[768,24]{1,0:T(8,128)(2,1)S(1)} %copy.17.wo_ref, ...), custom_call_target="tpu_custom_call" | custom-call | tf_op jit(solution)/shard_map/layer/pallas_call | solution.py:560
  111.1 0.6 copy.21
  (14 shorter events, 0.2 us)
Async XLA Ops:
  9.1 1.6 %copy-start = (bf16[5,256,768]{2,1,0:T(8,128)(2,1)S(1)}, bf16[5,256,768]{2,1,0:T(8,128)(2,1)}, u32[]{:S(2)}) copy-start(bf16[5,256,768]{2,1,0:T(8,128)(2,1)} %key_hbm.1) | copy-start | bytes 5898244
  10.7 1.5 %copy-start.1 = (bf16[5,256,768]{2,1,0:T(8,128)(2,1)S(1)}, bf16[5,256,768]{2,1,0:T(8,128)(2,1)}, u32[]{:S(2)}) copy-start(bf16[5,256,768]{2,1,0:T(8,128)(2,1)} %val_hbm.1) | copy-start | bytes 5898244
  12.2 0.9 copy-start.2
  13.1 0.7 copy-start.3
  13.8 0.7 copy-start.4

commit v2 on v1

v2 whole, which is shorter than its diff:
```python
import math

import jax
import jax.numpy as jnp
import numpy as np
from jax import lax
from jax.experimental import pallas as pl
from jax.experimental.pallas import tpu as pltpu
from jax.sharding import PartitionSpec as P

HD = 96
SCALE = 1.0 / math.sqrt(HD)
N = 8
X = 4
REQ = 256
DEV = 768
HALF = 384
BLK = 5
BT = 256
FFD = 64
MESH = pl.DeviceIdType.MESH
F32 = jnp.float32
BF16 = jnp.bfloat16


def tables():
    lane = np.arange(1024)
    s, r = lane // 128, lane % 128
    f, core, b = r // 10, (r // 5) % 2, r % 5
    ids = np.stack([((f * 16 + s * 2 + core) * 5 + b), ((s * 16 + f * 2 + core) * 5 + b)])
    ids = np.where(r[None] < 80, ids, -7).astype(np.float32)
    k = np.arange(768)
    s, f, core, i = k // 96, (k // 12) % 8, (k // 6) % 2, k % 6
    feats = []
    for z, y in ((f, s), (s, f)):
        feats.append(384 * (z % 2) + 48 * y + 24 * core + 6 * (z // 2) + i)
    out = np.zeros((8, 1024), np.float32)
    out[0:2] = ids
    out[2:4, :768] = np.stack(feats)
    half = np.arange(768) % 96
    power = -(2.0 * (half % 48)).astype(np.float32) / np.float32(96)
    out[4, :768] = np.float32(10000.0) ** power
    out[5, :768] = np.where(half < 48, -1.0, 1.0)
    return out


def nt(a, b):
    return lax.dot_general(a, b, (((1,), (1,)), ((), ())), preferred_element_type=F32)


def nn(a, b):
    return jnp.dot(a, b, preferred_element_type=F32)


def iota(shape, dim):
    return lax.broadcasted_iota(jnp.int32, shape, dim)


class Net:
    def __init__(self, send, recv):
        self.p = lax.axis_index("pool")
        self.x = lax.axis_index("mlp")
        self.c = self.p % 2
        self.y = (self.p // 2) % N
        self.z = self.p // (2 * N)
        c = self.c
        self.fi = self.z * (1 - c) + self.y * c
        self.si = self.y * (1 - c) + self.z * c
        self.sib = self.p + 1 - 2 * c
        self.send, self.recv = send, recv
        self.ns = self.nr = 0
        self.sent = []

    def recvs(self, count=1):
        base = self.nr
        self.nr += count
        return base

    def sends(self, ref=None):
        self.ns += 1
        if ref is not None:
            self.sent.append((ref, self.ns - 1))
        return self.ns - 1

    def chip(self, z, y, core):
        return z * (2 * N) + y * 2 + core

    def copy(self, src, dst, s, r, pool, mlp=None):
        return pltpu.make_async_remote_copy(
            src_ref=src,
            dst_ref=dst,
            send_sem=self.send.at[s],
            recv_sem=self.recv.at[r],
            device_id=(pool, self.x if mlp is None else mlp),
            device_id_type=MESH,
        )

    def put(self, *args):
        self.copy(*args).start()

    def got(self, dst, r):
        self.copy(dst, dst, 0, r, self.sib).wait_recv()

    def finish(self):
        for ref, s in self.sent:
            self.copy(ref, ref, s, 0, self.sib).wait_send()

    def spread(self, src, slots, r, along_first=True, pick=False):
        z, y, c = self.z, self.y, self.c
        own_index = self.fi if along_first else self.si
        s = self.sends(slots.at[pl.ds(0, 15)])
        for k in (4, 3, 5, 2, 6, 1, 7):
            for d in (0, 1):
                on_z = (d == 0) == along_first
                me = z if on_z else y
                t = (me + k) % N
                pool = self.chip(t, y, d) if on_z else self.chip(z, t, d)
                self.put(src.at[d, t] if pick else src.at[d], slots.at[me * 2 + c], s, r, pool)
        sib_index = self.si if along_first else self.fi
        part = src.at[1 - c, sib_index] if pick else src.at[1 - c]
        self.put(part, slots.at[sib_index * 2 + c], s, r, self.sib)
        slots[own_index * 2 + c] = src[c, own_index] if pick else src[c]

    def spread_wait(self, slots, r):
        self.got(slots.at[pl.ds(0, 15)], r)

    def line_open(self, view):
        return view, self.recvs(N), self.recvs(), self.sends(view(self.c, 0, 7)), self.sends(view(self.c, 0, 8))

    def line_send(self, *lines):
        c, si = self.c, self.si
        for k in (4, 3, 5, 2, 6, 1, 7):
            t = (si + k) % N
            pool = self.fi * (16 - 14 * c) + t * (2 + 14 * c) + c
            for view, r, _, s, _ in lines:
                self.put(view(c, si, 1), view(c, si, 1), s, r + si, pool)
        for view, _, r, _, s in lines:
            self.put(view(c, si, 1), view(c, si, 1), s, r, self.sib)

    def line_forward(self, *lines):
        c, si = self.c, self.si
        for k in (1, 7, 2, 6, 3, 5, 4):
            t = (si + k) % N
            for view, r, r2, _, s2 in lines:
                self.got(view(c, t, 1), r + t)
                self.put(view(c, t, 1), view(c, t, 1), s2, r2, self.sib)

    def line_wait(self, *lines):
        for view, _, r2, _, _ in lines:
            self.got(view(1 - self.c, 0, 8), r2)


def kernel(
    q_hbm, k_hbm, v_hbm, res_hbm, tab_hbm, len_hbm, const_hbm, wo_hbm, gain_hbm, gate_hbm, up_hbm,
    down_hbm, key_hbm, val_hbm, out_ref,
    q_ref, k_ref, v_ref, res_ref, tab_ref, len_ref, const_ref, wo_ref, gain_ref, gate_ref, up_ref,
    down_ref, kbuf, vbuf,
    pay, vr, slot1, slot2, line1, line2, g1, gv, gr,
    acc_src, lse_src, acc_slot, lse_slot, acc_line, ga, gl,
    bias, ebuf, attb, wgp, s3_src, s3_slot, h_src, h_slot, h_line, gh,
    gu_buf, sq_buf, dbuf, d_slot, b_src, b_slot,
    send, recv, local,
):
    net = Net(send, recv)
    p, x, c, y, z, fi, si = net.p, net.x, net.c, net.y, net.z, net.fi, net.si
    group = p // 32
    rest = p % 32

    pairs = [
        (len_hbm, len_ref), (q_hbm, q_ref), (k_hbm, k_ref), (tab_hbm, tab_ref),
        (const_hbm, const_ref), (v_hbm, v_ref), (res_hbm, res_ref), (gate_hbm, gate_ref),
        (up_hbm, up_ref), (gain_hbm, gain_ref), (wo_hbm, wo_ref), (down_hbm, down_ref),
        (key_hbm, kbuf), (val_hbm, vbuf),
    ]
    loads = [pltpu.make_async_copy(a, b, local.at[i]) for i, (a, b) in enumerate(pairs)]
    for load in loads:
        load.start()

    barrier = pltpu.get_barrier_semaphore()

    def hello(pool, mlp):
        pl.semaphore_signal(barrier, inc=1, device_id=(pool, mlp), device_id_type=MESH)

    for k in range(1, N):
        for e in (0, 1):
            hello(net.chip((z + k) % N, y, e), x)
            hello(net.chip(z, (y + k) % N, e), x)
    hello(net.sib, x)
    for k in range(1, X):
        hello(p, (x + k) % X)
    home = group == x
    for k in range(X):

        @pl.when(jnp.logical_not(jnp.logical_and(home, x == k)))
        def _():
            hello(32 * x + rest, k)

    for load in loads[:7]:
        load.wait()
    row8 = iota((8, DEV), 0)
    where_len = jnp.where(row8 == 0, len_ref[0], len_ref[1]).astype(F32)
    angle = where_len * const_ref[4:5, :DEV]
    sign = jnp.broadcast_to(const_ref[5:6, :DEV], (8, DEV))
    cosine, sine = jnp.cos(angle), jnp.sin(angle) * sign
    turned = []
    for ref in (q_ref, k_ref):
        value = jnp.concatenate([ref[...].astype(F32), jnp.zeros((6, DEV), F32)], 0)
        other = jnp.where(
            sign < 0.0, pltpu.roll(value, DEV - HD // 2, 1), pltpu.roll(value, HD // 2, 1)
        )
        turned.append((value * cosine + other * sine).astype(BF16).astype(F32))
    product = turned[0] * turned[1]
    col8 = iota((8, DEV), 1)
    lane128 = iota((8, 128), 1)
    row128 = iota((8, 128), 0)
    lists = jnp.zeros((8, 128), F32)
    for i in (0, 1):
        for j in range(9):
            value = len_ref[i] if j == 8 else tab_ref[i, j]
            here = jnp.logical_and(row128 == i, lane128 == j)
            lists = jnp.where(here, (value >> 4).astype(F32), lists)
            here = jnp.logical_and(row128 == i, lane128 == 16 + j)
            lists = jnp.where(here, (value & 15).astype(F32), lists)
    for d in (0, 1):
        meta = lists
        for h in range(4):
            head = 4 * d + h
            inside = jnp.logical_and(col8 >= HD * head, col8 < HD * head + HD)
            score = jnp.sum(jnp.where(inside, product, 0.0), 1, keepdims=True) * SCALE
            for t in range(3):
                part = score.astype(BF16).astype(F32)
                meta = jnp.where(lane128 == 32 + 4 * t + h, part, meta)
                score = score - part
        pay[d, :, :HALF] = turned[0][0:2, HALF * d : HALF * d + HALF].astype(BF16)
        pay[d, :, HALF:] = meta[0:2].astype(BF16)
        vr[d, :, :HALF] = v_ref[:, HALF * d : HALF * d + HALF]
        vr[d, :, HALF:] = res_ref[:, HALF * d : HALF * d + HALF]

    pl.semaphore_wait(barrier, 36 - jnp.where(home, 1, 0))

    r_pay, r_vr = net.recvs(), net.recvs()
    net.spread(pay, slot1, r_pay)
    net.spread(vr, slot2, r_vr)
    q_line = net.line_open(lambda d, s, n: g1.at[d, pl.ds(s, n)])
    v_line = net.line_open(lambda d, s, n: gv.at[d, pl.ds(s, n)])
    r_line = net.line_open(lambda d, s, n: gr.at[d, pl.ds(s, n)])

    for load in loads[7:]:
        load.wait()
    gain = gain_ref[...].astype(F32)
    wg = jnp.concatenate([gate_ref[...].astype(F32), up_ref[...].astype(F32)], 0)
    wg = (wg * gain).astype(BF16)
    for d in (0, 1):
        feat = const_ref[2 + d : 3 + d, :DEV]
        for g in range(6):
            cols = feat[:, 128 * g : 128 * g + 128]
            place = (iota((DEV, 128), 0).astype(F32) == cols).astype(F32).astype(BF16)
            wgp[d, :, 128 * g : 128 * g + 128] = nn(wg, place).astype(BF16)
    wot = wo_ref[...]
    o_row, n_col = iota((REQ, REQ), 0), iota((REQ, REQ), 1)
    nat_row = ((o_row >> 2) & 7) * 32 + (o_row >> 5) * 4 + (o_row & 3)
    nat_col = ((n_col >> 2) & 7) * 32 + (n_col >> 5) * 4 + (n_col & 3)
    to_order0 = (nat_row == n_col).astype(F32).astype(BF16)
    to_natural = (o_row == nat_col).astype(F32).astype(BF16)

    net.spread_wait(slot1, r_pay)
    for j in range(16):
        line1[2 * j : 2 * j + 2, :] = slot1[j].astype(F32)
    g1[c, si] = line1[...].astype(BF16)
    net.line_send(q_line)
    net.spread_wait(slot2, r_vr)
    for j in range(16):
        line2[2 * j : 2 * j + 2, :] = slot2[j].astype(F32)
    gv[c, si] = line2[:, :HALF].astype(BF16)
    gr[c, si] = line2[:, HALF:].astype(BF16)
    net.line_forward(q_line)
    net.line_send(v_line)
    net.line_wait(q_line)

    metas = []
    queries = []
    own_len = None
    sub8 = iota((8, REQ), 0)
    for d in (0, 1):
        meta = g1[d, :, :, HALF:].reshape(REQ, 128).astype(F32)
        metas.append(meta)
        meta_t = meta.T
        tab = 16.0 * meta_t[0:16] + meta_t[16:32]
        onehot = jnp.zeros((8, REQ), F32)
        lens = []
        for b in range(BLK):
            match = (tab[0:8] == (p * BLK + b).astype(F32)).astype(F32)
            row = jnp.max(match, 0, keepdims=True)
            onehot = jnp.where(sub8 == b, row, onehot)
            left = match * (tab[8:9] - 256.0 * sub8.astype(F32))
            lens.append(jnp.sum(jnp.sum(left, 0, keepdims=True), 1, keepdims=True))
        own_len = lens
        queries.append(nn(onehot.astype(BF16), g1[d, :, :, :HALF].reshape(REQ, HALF)))
    lane = iota((8, DEV), 1)
    sub = iota((8, DEV), 0)
    head_mask = jnp.logical_and(lane >= 96 * sub, lane < 96 * sub + 96)
    query = jnp.concatenate(queries, 1)
    acc = jnp.zeros((8, DEV), F32)
    tiles = [jnp.zeros((8, 128), F32), jnp.zeros((8, 128), F32)]
    for b in range(BLK):
        wide = jnp.where(head_mask, query[b : b + 1, :], 0.0).astype(BF16)
        scores = nt(wide, kbuf[b]) * SCALE
        valid = iota((8, BT), 1).astype(F32) < own_len[b]
        scores = jnp.where(valid, scores, -1e30)
        top = jnp.max(scores, 1, keepdims=True)
        weights = jnp.where(valid, jnp.exp(scores - top), 0.0)
        total = jnp.maximum(jnp.sum(weights, 1, keepdims=True), 1.0)
        numer = nn(weights.astype(BF16), vbuf[b]) / total
        row = jnp.sum(jnp.where(head_mask, numer, 0.0), 0, keepdims=True)
        acc = jnp.where(sub == b, row, acc)
        lse = top + jnp.log(total)
        for d, f in ((0, z), (1, y)):
            tiles[d] = jnp.where(lane128 == 10 * f + 5 * c + b, lse, tiles[d])
    for d in (0, 1):
        acc_src[d] = acc[:, HALF * d : HALF * d + HALF].astype(BF16)
        lse_src[d] = tiles[d]

    r_acc, r_lse = net.recvs(), net.recvs()
    net.spread(acc_src, acc_slot, r_acc)
    net.spread(lse_src, lse_slot, r_lse)
    a_lines = (
        net.line_open(lambda d, s, n: ga.at[d, pl.ds(s, n), pl.ds(0, 80)]),
        net.line_open(lambda d, s, n: gl.at[d, pl.ds(s, n)]),
    )
    for d in (0, 1):
        meta = metas[d]
        cols = [16.0 * meta[:, j : j + 1] + meta[:, 16 + j : 17 + j] for j in range(8)]
        for s in range(N):
            ids = const_ref[d : d + 1, 128 * s : 128 * s + 128]
            hit = cols[0] == ids
            for j in range(1, 8):
                hit = jnp.logical_or(hit, cols[j] == ids)
            bias[d, :, 128 * s : 128 * s + 128] = jnp.where(hit, 0.0, -1e30)
            ga[d, s, 80:128, :] = jnp.zeros((48, HALF), BF16)
    net.spread_wait(acc_slot, r_acc)
    for j in range(16):
        acc_line[5 * j : 5 * j + 5, :] = acc_slot[j].astype(F32)[0:5]
    ga[c, si, 0:80, :] = acc_line[...].astype(BF16)
    net.spread_wait(lse_slot, r_lse)
    line = lse_slot[0]
    for j in range(1, 16):
        line = line + lse_slot[j]
    gl[c, si] = line
    net.line_send(*a_lines)
    net.line_forward(v_line)
    net.line_forward(*a_lines)
    net.line_send(r_line)
    net.line_wait(v_line)
    net.line_wait(*a_lines)

    for d in (0, 1):
        meta = metas[d]
        selfs, totals = [], []
        for h in range(4):
            own = meta[:, 32 + h : 33 + h] + meta[:, 36 + h : 37 + h] + meta[:, 40 + h : 41 + h]
            row = 4 * d + h
            score = jnp.concatenate([gl[d, s, row : row + 1, :] for s in range(N)], 1)
            logits = score + bias[d]
            top = jnp.maximum(jnp.max(logits, 1, keepdims=True), own)
            weights = jnp.exp(logits - top)
            own_weight = jnp.exp(own - top)
            totals.append(jnp.sum(weights, 1, keepdims=True) + own_weight)
            selfs.append(own_weight.astype(BF16).astype(F32))
            ebuf[h] = weights.astype(BF16)
        lane_r = iota((REQ, 128), 1)
        for g in range(3):
            block = ga[d, :, :, 128 * g : 128 * g + 128].reshape(1024, 128)
            low = lane_r < 96 - 32 * g
            numer = jnp.where(low, nn(ebuf[g], block), nn(ebuf[g + 1], block))
            value = gv[d, :, :, 128 * g : 128 * g + 128].reshape(REQ, 128).astype(F32)
            numer = numer + jnp.where(low, selfs[g], selfs[g + 1]) * value
            attb[d, :, 128 * g : 128 * g + 128] = (
                numer / jnp.where(low, totals[g], totals[g + 1])
            ).astype(BF16)
    att0 = nn(to_natural, attb[0]).astype(BF16)
    head = nt(wot[:, :HALF], att0) + nt(wot[:, HALF:], attb[1])

    r_s3 = net.recvs(X)
    for k in range(X):
        s3_src[k] = head[6 * k : 6 * k + 6]
    copies = []
    for k in range(X):
        is_self = jnp.logical_and(home, x == k)
        copies.append(
            net.copy(
                s3_src.at[k], s3_slot.at[x], net.sends(), r_s3 + x, 32 * k + rest, group
            )
        )

        @pl.when(jnp.logical_not(is_self))
        def _(k=k):
            copies[k].start()

    @pl.when(home)
    def _():
        s3_slot[x] = s3_src[x]

    net.line_forward(r_line)
    net.line_wait(r_line)
    feature = 24 * rest + 6 * group + iota((8, HALF), 0)
    inputs = []
    for d in (0, 1):
        pick = jnp.logical_and(
            iota((8, HALF), 1) + HALF * d == feature, iota((8, HALF), 0) < 6
        )
        inputs.append(nt(pick.astype(F32).astype(BF16), gr[d].reshape(REQ, HALF)))
    piece = nt(inputs[0].astype(BF16), to_natural) + inputs[1]
    for k in range(X):

        @pl.when(jnp.logical_not(jnp.logical_and(home, x == k)))
        def _(k=k):
            net.got(s3_slot.at[k], r_s3 + k)

    total = (s3_slot[0] + s3_slot[1]) + (s3_slot[2] + s3_slot[3])
    piece = piece[0:6] + total.astype(BF16).astype(F32)
    h_src[0] = piece[:, :128]
    h_src[1] = piece[:, 128:]

    r_h = net.recvs()
    net.spread(h_src, h_slot, r_h)
    h_lines = net.line_open(lambda d, s, n: gh.at[d, pl.ds(s, n)])
    net.spread_wait(h_slot, r_h)
    for j in range(16):
        h_line[6 * j : 6 * j + 6, :] = h_slot[j]
    gh[c, si] = h_line[...].astype(BF16)
    net.line_send(h_lines)
    net.line_forward(h_lines)
    net.line_wait(h_lines)

    for d in (0, 1):
        resid = gh[d].reshape(DEV, 128)
        gu_buf[x, :, 128 * d : 128 * d + 128] = nn(wgp[d], resid).astype(BF16)
        wide = resid.astype(F32)
        square = jnp.sum(wide * wide, 0, keepdims=True)
        sq_buf[x, :, 128 * d : 128 * d + 128] = jnp.broadcast_to(square, (8, 128))
    r_gu, r_sq = net.recvs(), net.recvs()
    s_gu, s_sq = net.sends(gu_buf.at[pl.ds(0, 3)]), net.sends(sq_buf.at[pl.ds(0, 3)])
    for k in (2, 1, 3):
        net.put(gu_buf.at[x], gu_buf.at[x], s_gu, r_gu, p, (x + k) % X)
        net.put(sq_buf.at[x], sq_buf.at[x], s_sq, r_sq, p, (x + k) % X)
    own_resid = jnp.zeros((8, DEV), F32)
    for d in (0, 1):
        pick = iota((8, 128), 1) + 128 * d == 2 * p + iota((8, 128), 0)
        pick = jnp.logical_and(pick, iota((8, 128), 0) < 2)
        mine = nt(pick.astype(F32).astype(BF16), gh[d].reshape(DEV, 128)).astype(BF16)
        feat = const_ref[2 + d : 3 + d, :DEV]
        parts = []
        for g in range(6):
            place = iota((128, DEV), 0).astype(F32) + 128.0 * g == feat
            parts.append(nt(mine, place.astype(F32).astype(BF16)))
        own_resid = own_resid + jnp.concatenate(parts, 1)
    net.got(gu_buf.at[pl.ds(0, 3)], r_gu)
    net.got(sq_buf.at[pl.ds(0, 3)], r_sq)
    gu = gu_buf[0].astype(F32)
    square = sq_buf[0]
    for k in range(1, X):
        gu = gu + gu_buf[k].astype(F32)
        square = square + sq_buf[k]
    inv = lax.rsqrt(square[0:1] * (1.0 / (X * DEV)) + 1e-05)
    gate = gu[:FFD] * inv
    up = gu[FFD:] * inv
    hidden = gate / (1.0 + jnp.exp(-gate)) * up
    hidden_t = hidden.T.astype(BF16)

    down = down_ref[...]
    rows = [nn(to_order0, hidden_t).astype(BF16), hidden_t]
    for d in (0, 1):
        part = nn(rows[d], down[:, HALF * d : HALF * d + HALF]).astype(BF16)
        for s in range(N):
            dbuf[d, s] = part[32 * s : 32 * s + 32]
    r_d = net.recvs()
    net.spread(dbuf, d_slot, r_d, along_first=False, pick=True)
    net.spread_wait(d_slot, r_d)
    part = d_slot[0].astype(F32)
    for j in range(1, 16):
        part = part + d_slot[j].astype(F32)
    for f in range(N):
        for e in (0, 1):
            b_src[f, e] = part[4 * f + 2 * e : 4 * f + 2 * e + 2]
    r_b = net.recvs()
    s_b = net.sends(b_slot.at[pl.ds(0, 15)])
    own = c * N + fi
    for k in (4, 3, 5, 2, 6, 1, 7):
        t = (fi + k) % N
        for e in (0, 1):
            pool = net.chip(t * (1 - c) + z * c, y * (1 - c) + t * c, e)
            net.put(b_src.at[t, e], b_slot.at[own], s_b, r_b, pool)
    net.put(b_src.at[fi, 1 - c], b_slot.at[own], s_b, r_b, net.sib)
    b_slot[own] = b_src[fi, c]
    net.got(b_slot.at[pl.ds(0, 15)], r_b)
    for d in (0, 1):
        total = b_slot[N * d]
        for f in range(1, N):
            total = total + b_slot[N * d + f]
        out_ref[:, HALF * d : HALF * d + HALF] = (
            own_resid[0:2, HALF * d : HALF * d + HALF] + total
        ).astype(BF16)

    net.finish()
    for k in range(X):

        @pl.when(jnp.logical_not(jnp.logical_and(home, x == k)))
        def _(k=k):
            copies[k].wait_send()


SENDS = 32
RECVS = 72


def scratch():
    v = pltpu.VMEM
    return [
        v((2, DEV), BF16), v((2, DEV), BF16), v((2, DEV), BF16), v((2, DEV), BF16),
        pltpu.SMEM((2, 8), jnp.int32), pltpu.SMEM((2,), jnp.int32), v((8, 1024), F32),
        v((24, DEV), BF16), v((1, DEV), BF16), v((FFD, DEV), BF16), v((FFD, DEV), BF16),
        v((FFD, DEV), BF16), v((BLK, BT, DEV), BF16), v((BLK, BT, DEV), BF16),
        v((2, 2, 512), BF16), v((2, 2, DEV), BF16),
        v((16, 2, 512), BF16), v((16, 2, DEV), BF16), v((32, 512), F32), v((32, DEV), F32),
        v((2, N, 32, 512), BF16), v((2, N, 32, HALF), BF16), v((2, N, 32, HALF), BF16),
        v((2, 8, HALF), BF16), v((2, 8, 128), F32), v((16, 8, HALF), BF16), v((16, 8, 128), F32),
        v((80, HALF), F32), v((2, N, 128, HALF), BF16), v((2, N, 8, 128), F32),
        v((2, REQ, 1024), F32), v((4, REQ, 1024), BF16), v((2, REQ, HALF), BF16),
        v((2, 128, DEV), BF16),
        v((X, 6, REQ), F32), v((X, 6, REQ), F32),
        v((2, 6, 128), F32), v((16, 6, 128), F32), v((96, 128), F32), v((2, N, 96, 128), BF16),
        v((X, 128, REQ), BF16), v((X, 8, REQ), F32),
        v((2, N, 32, HALF), BF16), v((16, 32, HALF), BF16), v((N, 2, 2, HALF), F32), v((16, 2, HALF), F32),
        pltpu.SemaphoreType.DMA((SENDS,)), pltpu.SemaphoreType.DMA((RECVS,)),
        pltpu.SemaphoreType.DMA((14,)),
    ]


def per_device(
    residual_in, query_new, key_new, value_new, key_cache, value_cache, block_table, lengths,
    out_weight, norm_gain, gate_weight, up_weight, down_weight,
):
    vm = pl.BlockSpec(memory_space=pltpu.VMEM)
    hbm = pl.BlockSpec(memory_space=pl.ANY)
    return pl.pallas_call(
        kernel,
        out_shape=jax.ShapeDtypeStruct((2, DEV), BF16),
        in_specs=[hbm] * 14,
        out_specs=vm,
        scratch_shapes=scratch(),
        compiler_params=pltpu.CompilerParams(
            collective_id=0, has_side_effects=True, vmem_limit_bytes=60 * 1024 * 1024
        ),
        name="layer",
    )(
        query_new, key_new, value_new, residual_in, block_table, lengths, jnp.asarray(tables()),
        out_weight.T, norm_gain.reshape(1, DEV), gate_weight.T, up_weight.T, down_weight,
        key_cache, value_cache,
    )


def solution(mesh):
    in_specs = (
        P("pool", "mlp"),
        P("pool", "mlp"),
        P("pool", "mlp"),
        P("pool", "mlp"),
        P("pool", None, "mlp"),
        P("pool", None, "mlp"),
        P("pool", None),
        P("pool"),
        P("mlp", "pool"),
        P("mlp"),
        P("mlp", "pool"),
        P("mlp", "pool"),
        P("pool", "mlp"),
    )
    out_specs = P("pool", "mlp")
    return jax.shard_map(
        per_device, mesh=mesh, in_specs=in_specs, out_specs=out_specs, check_vma=False
    )
```

time: 112 us -> 87.4 us (0.78)
  Pallas kernels: 96.6 us -> 84.7 us
  local copies, waits for them, and re-layouts: 13.1 us -> 2.53 us
  other arithmetic: 1.88 us -> 0 us
    pallas_call x1, Pallas kernels: 96.6 us -> 84.7 us  [per_device(): pl.pallas_call(kernel, out_shape=jax.ShapeDtypeStruct((2, DEV), BF16), in...]
    unnamed x14 -> x1, local copies, waits for them, and re-layouts: 9 us -> 1.26 us
    reshape x2 -> x0, local copies, waits for them, and re-layouts: 1.53 us -> none  [the longest x1 0.77 us: per_device(): query_new.astype(F32).reshape(2, heads, HD)]
    convert_element_type x2 -> x0, other arithmetic: 1.41 us -> none  [the longest x1 0.75 us: per_device(): low = (whole & 15).astype(F32)]
where the time goes in v2:
time: 87.4 us; the launch traced here: 87.2 us
  Pallas kernels  84.7 us (97%)
  local copies, waits for them, and re-layouts  2.53 us (3%)
    pallas_call x1, Pallas kernels, per_device(): pl.pallas_call(kernel, out_shape=jax.ShapeDtypeStruct((2, DEV), BF16), in...  84.7 us

profile of v2, /device:TPU:1, one launch (start us, length us, event | category | flops | bytes accessed | tf_op | source)
XLA Modules:
  0.0 87.2 jit_solution(8317145883433674518)
XLA Ops:
  0.0 1.3 %reshape.3.gain_hbm = bf16[1,768]{1,0:T(2,128)(2,1)} reshape(bf16[768]{0:T(1024)(128)(2,1)} %param.23) | data formatting | bytes 3072 | tf_op jit(solution)/shard_map/reshape | solution.py:557
  1.3 84.7 %layer.1 = bf16[2,768]{1,0:T(2,128)(2,1)} custom-call(bf16[2,768]{1,0:T(2,128)(2,1)} %q_hbm.1, bf16[2,768]{1,0:T(2,128)(2,1)} %k_hbm.1, bf16[2,768]{1,0:T(2,128)(2,1)} %v_hbm.1, bf16[2,768]{1,0:T(2,128)(2,1)} %res_hbm.1, s32[2,8]{1,0:T(2,128)} %tab_hbm.1, s32[2]{0:T(128)} %len_hbm.1, f32[8,1024]{1,0:T(8,128)} %constant.2.clone.const_hbm, ...), custom_call_target="tpu_custom_call" | custom-call | tf_op jit(solution)/shard_map/layer/pallas_call | solution.py:545
  86.0 1.3 %copy.16 = bf16[2,768]{1,0:T(2,128)(2,1)} copy(bf16[2,768]{1,0:T(2,128)(2,1)} %layer.1) | data formatting | bytes 6144

commit v3 on v2

--- a/solution.py
+++ b/solution.py
@@ -29,19 +29,26 @@
     f, core, b = r // 10, (r // 5) % 2, r % 5
     ids = np.stack([((f * 16 + s * 2 + core) * 5 + b), ((s * 16 + f * 2 + core) * 5 + b)])
     ids = np.where(r[None] < 80, ids, -7).astype(np.float32)
-    k = np.arange(768)
-    s, f, core, i = k // 96, (k // 12) % 8, (k // 6) % 2, k % 6
-    feats = []
-    for z, y in ((f, s), (s, f)):
-        feats.append(384 * (z % 2) + 48 * y + 24 * core + 6 * (z // 2) + i)
+    z, y, i = lane // 128, (lane // 16) % 8, lane % 16
+    feats = 384 * (z % 2) + 48 * y + 24 * ((z // 2) % 2) + 12 * (z // 4) + i
+    feats = np.where(i < 12, feats, -7)
     out = np.zeros((8, 1024), np.float32)
     out[0:2] = ids
-    out[2:4, :768] = np.stack(feats)
+    out[2] = feats
     half = np.arange(768) % 96
     power = -(2.0 * (half % 48)).astype(np.float32) / np.float32(96)
     out[4, :768] = np.float32(10000.0) ** power
     out[5, :768] = np.where(half < 48, -1.0, 1.0)
     return out
+
+
+def hops(k):
+    return min(k, N - k)
+
+
+FAR = sorted(
+    [(a, b) for a in range(N) for b in range(N) if a or b], key=lambda k: -hops(k[0]) - hops(k[1])
+)
 
 
 def nt(a, b):
@@ -105,21 +112,17 @@
         for ref, s in self.sent:
             self.copy(ref, ref, s, 0, self.sib).wait_send()
 
-    def spread(self, src, slots, r, along_first=True, pick=False):
+    def spread(self, src, slots, r):
         z, y, c = self.z, self.y, self.c
-        own_index = self.fi if along_first else self.si
         s = self.sends(slots.at[pl.ds(0, 15)])
         for k in (4, 3, 5, 2, 6, 1, 7):
             for d in (0, 1):
-                on_z = (d == 0) == along_first
-                me = z if on_z else y
+                me = y if d else z
                 t = (me + k) % N
-                pool = self.chip(t, y, d) if on_z else self.chip(z, t, d)
-                self.put(src.at[d, t] if pick else src.at[d], slots.at[me * 2 + c], s, r, pool)
-        sib_index = self.si if along_first else self.fi
-        part = src.at[1 - c, sib_index] if pick else src.at[1 - c]
-        self.put(part, slots.at[sib_index * 2 + c], s, r, self.sib)
-        slots[own_index * 2 + c] = src[c, own_index] if pick else src[c]
+                pool = self.chip(z, t, d) if d else self.chip(t, y, d)
+                self.put(src.at[d], slots.at[me * 2 + c], s, r, pool)
+        self.put(src.at[1 - c], slots.at[self.si * 2 + c], s, r, self.sib)
+        slots[self.fi * 2 + c] = src[c]
 
     def spread_wait(self, slots, r):
         self.got(slots.at[pl.ds(0, 15)], r)
@@ -137,9 +140,9 @@
         for view, _, r, _, s in lines:
             self.put(view(c, si, 1), view(c, si, 1), s, r, self.sib)
 
-    def line_forward(self, *lines):
+    def line_forward(self, *lines, steps=(1, 7, 2, 6, 3, 5, 4)):
         c, si = self.c, self.si
-        for k in (1, 7, 2, 6, 3, 5, 4):
+        for k in steps:
             t = (si + k) % N
             for view, r, r2, _, s2 in lines:
                 self.got(view(c, t, 1), r + t)
@@ -157,14 +160,13 @@
     down_ref, kbuf, vbuf,
     pay, vr, slot1, slot2, line1, line2, g1, gv, gr,
     acc_src, lse_src, acc_slot, lse_slot, acc_line, ga, gl,
-    bias, ebuf, attb, wgp, s3_src, s3_slot, h_src, h_slot, h_line, gh,
+    bias, ebuf, attb, wgp, place, s3_src, s3_slot, g4,
     gu_buf, sq_buf, dbuf, d_slot, b_src, b_slot,
     send, recv, local,
 ):
     net = Net(send, recv)
     p, x, c, y, z, fi, si = net.p, net.x, net.c, net.y, net.z, net.fi, net.si
     group = p // 32
-    rest = p % 32
 
     pairs = [
         (len_hbm, len_ref), (q_hbm, q_ref), (k_hbm, k_ref), (tab_hbm, tab_ref),
@@ -188,12 +190,13 @@
     hello(net.sib, x)
     for k in range(1, X):
         hello(p, (x + k) % X)
-    home = group == x
+    source = 32 * x + 16 * (z % 2) + 2 * y + group % 2
+    home = jnp.logical_and(group == x, group % 2 == c)
     for k in range(X):
 
         @pl.when(jnp.logical_not(jnp.logical_and(home, x == k)))
         def _():
-            hello(32 * x + rest, k)
+            hello(source, k)
 
     for load in loads[:7]:
         load.wait()
@@ -245,22 +248,10 @@
     v_line = net.line_open(lambda d, s, n: gv.at[d, pl.ds(s, n)])
     r_line = net.line_open(lambda d, s, n: gr.at[d, pl.ds(s, n)])
 
-    for load in loads[7:]:
-        load.wait()
-    gain = gain_ref[...].astype(F32)
-    wg = jnp.concatenate([gate_ref[...].astype(F32), up_ref[...].astype(F32)], 0)
-    wg = (wg * gain).astype(BF16)
-    for d in (0, 1):
-        feat = const_ref[2 + d : 3 + d, :DEV]
-        for g in range(6):
-            cols = feat[:, 128 * g : 128 * g + 128]
-            place = (iota((DEV, 128), 0).astype(F32) == cols).astype(F32).astype(BF16)
-            wgp[d, :, 128 * g : 128 * g + 128] = nn(wg, place).astype(BF16)
-    wot = wo_ref[...]
     o_row, n_col = iota((REQ, REQ), 0), iota((REQ, REQ), 1)
-    nat_row = ((o_row >> 2) & 7) * 32 + (o_row >> 5) * 4 + (o_row & 3)
+    nat_row = ((o_row >> 1) & 63) * 4 + (o_row >> 7) * 2 + (o_row & 1)
     nat_col = ((n_col >> 2) & 7) * 32 + (n_col >> 5) * 4 + (n_col & 3)
-    to_order0 = (nat_row == n_col).astype(F32).astype(BF16)
+    to_core = (nat_row == n_col).astype(F32).astype(BF16)
     to_natural = (o_row == nat_col).astype(F32).astype(BF16)
 
     net.spread_wait(slot1, r_pay)
@@ -300,6 +291,8 @@
     sub = iota((8, DEV), 0)
     head_mask = jnp.logical_and(lane >= 96 * sub, lane < 96 * sub + 96)
     query = jnp.concatenate(queries, 1)
+    for load in loads[7:]:
+        load.wait()
     acc = jnp.zeros((8, DEV), F32)
     tiles = [jnp.zeros((8, 128), F32), jnp.zeros((8, 128), F32)]
     for b in range(BLK):
@@ -346,70 +339,74 @@
     for j in range(1, 16):
         line = line + lse_slot[j]
     gl[c, si] = line
-    net.line_send(*a_lines)
+    net.line_send(a_lines[1])
+    net.line_send(a_lines[0])
+    net.line_forward(a_lines[1])
     net.line_forward(v_line)
-    net.line_forward(*a_lines)
+    net.line_wait(a_lines[1])
+
+    selfs, totals = [], []
+    steps = ((1,), (7,), (2,), (6,), (3,), (5,), (4,), ())
+    for row in range(8):
+        d, h = row // 4, row % 4
+        meta = metas[d]
+        own = meta[:, 32 + h : 33 + h] + meta[:, 36 + h : 37 + h] + meta[:, 40 + h : 41 + h]
+        score = jnp.concatenate([gl[d, s, row : row + 1, :] for s in range(N)], 1)
+        logits = score + bias[d]
+        top = jnp.maximum(jnp.max(logits, 1, keepdims=True), own)
+        weights = jnp.exp(logits - top)
+        own_weight = jnp.exp(own - top)
+        totals.append(jnp.sum(weights, 1, keepdims=True) + own_weight)
+        selfs.append(own_weight.astype(BF16).astype(F32))
+        ebuf[row] = weights.astype(BF16)
+        net.line_forward(a_lines[0], steps=steps[row])
     net.line_send(r_line)
-    net.line_wait(v_line)
-    net.line_wait(*a_lines)
-
-    for d in (0, 1):
-        meta = metas[d]
-        selfs, totals = [], []
-        for h in range(4):
-            own = meta[:, 32 + h : 33 + h] + meta[:, 36 + h : 37 + h] + meta[:, 40 + h : 41 + h]
-            row = 4 * d + h
-            score = jnp.concatenate([gl[d, s, row : row + 1, :] for s in range(N)], 1)
-            logits = score + bias[d]
-            top = jnp.maximum(jnp.max(logits, 1, keepdims=True), own)
-            weights = jnp.exp(logits - top)
-            own_weight = jnp.exp(own - top)
-            totals.append(jnp.sum(weights, 1, keepdims=True) + own_weight)
-            selfs.append(own_weight.astype(BF16).astype(F32))
-            ebuf[h] = weights.astype(BF16)
+    net.line_wait(v_line, a_lines[0])
+
+    for d in (0, 1):
         lane_r = iota((REQ, 128), 1)
         for g in range(3):
             block = ga[d, :, :, 128 * g : 128 * g + 128].reshape(1024, 128)
             low = lane_r < 96 - 32 * g
-            numer = jnp.where(low, nn(ebuf[g], block), nn(ebuf[g + 1], block))
+            i = 4 * d + g
+            numer = jnp.where(low, nn(ebuf[i], block), nn(ebuf[i + 1], block))
             value = gv[d, :, :, 128 * g : 128 * g + 128].reshape(REQ, 128).astype(F32)
-            numer = numer + jnp.where(low, selfs[g], selfs[g + 1]) * value
+            numer = numer + jnp.where(low, selfs[i], selfs[i + 1]) * value
             attb[d, :, 128 * g : 128 * g + 128] = (
-                numer / jnp.where(low, totals[g], totals[g + 1])
+                numer / jnp.where(low, totals[i], totals[i + 1])
             ).astype(BF16)
     att0 = nn(to_natural, attb[0]).astype(BF16)
-    head = nt(wot[:, :HALF], att0) + nt(wot[:, HALF:], attb[1])
+    head = nt(wo_ref[:, :HALF], att0) + nt(wo_ref[:, HALF:], attb[1])
 
     r_s3 = net.recvs(X)
-    for k in range(X):
-        s3_src[k] = head[6 * k : 6 * k + 6]
     copies = []
     for k in range(X):
-        is_self = jnp.logical_and(home, x == k)
-        copies.append(
-            net.copy(
-                s3_src.at[k], s3_slot.at[x], net.sends(), r_s3 + x, 32 * k + rest, group
-            )
-        )
-
-        @pl.when(jnp.logical_not(is_self))
+        a, b = k // 2, k % 2
+        s3_src[k] = head[12 * a : 12 * a + 12, 128 * b : 128 * b + 128]
+        pool = net.chip(z % 2 + 2 * c + 4 * a, y, b)
+        copies.append(net.copy(s3_src.at[k], s3_slot.at[x], net.sends(), r_s3 + x, pool, group))
+    kept = 2 * (z // 4) + c
+    for k in range(X):
+
+        @pl.when(jnp.logical_not(jnp.logical_and(home, kept == k)))
         def _(k=k):
             copies[k].start()
 
     @pl.when(home)
     def _():
-        s3_slot[x] = s3_src[x]
+        s3_slot[x] = s3_src[kept]
 
     net.line_forward(r_line)
     net.line_wait(r_line)
-    feature = 24 * rest + 6 * group + iota((8, HALF), 0)
+    feature = 384 * (z % 2) + 48 * y + 24 * (group % 2) + 12 * (z // 4) + iota((16, HALF), 0)
     inputs = []
     for d in (0, 1):
         pick = jnp.logical_and(
-            iota((8, HALF), 1) + HALF * d == feature, iota((8, HALF), 0) < 6
+            iota((16, HALF), 1) + HALF * d == feature, iota((16, HALF), 0) < 12
         )
         inputs.append(nt(pick.astype(F32).astype(BF16), gr[d].reshape(REQ, HALF)))
     piece = nt(inputs[0].astype(BF16), to_natural) + inputs[1]
+    piece = jnp.where(c == 0, piece[:, :128], piece[:, 128:])
     for k in range(X):
 
         @pl.when(jnp.logical_not(jnp.logical_and(home, x == k)))
@@ -417,24 +414,33 @@
             net.got(s3_slot.at[k], r_s3 + k)
 
     total = (s3_slot[0] + s3_slot[1]) + (s3_slot[2] + s3_slot[3])
-    piece = piece[0:6] + total.astype(BF16).astype(F32)
-    h_src[0] = piece[:, :128]
-    h_src[1] = piece[:, 128:]
-
-    r_h = net.recvs()
-    net.spread(h_src, h_slot, r_h)
-    h_lines = net.line_open(lambda d, s, n: gh.at[d, pl.ds(s, n)])
-    net.spread_wait(h_slot, r_h)
-    for j in range(16):
-        h_line[6 * j : 6 * j + 6, :] = h_slot[j]
-    gh[c, si] = h_line[...].astype(BF16)
-    net.line_send(h_lines)
-    net.line_forward(h_lines)
-    net.line_wait(h_lines)
-
-    for d in (0, 1):
-        resid = gh[d].reshape(DEV, 128)
-        gu_buf[x, :, 128 * d : 128 * d + 128] = nn(wgp[d], resid).astype(BF16)
+    total = jnp.concatenate([total.astype(BF16).astype(F32), jnp.zeros((4, 128), F32)], 0)
+    me = z * N + y
+    g4[c, me] = (piece + total).astype(BF16)
+
+    r_h, r_h2 = net.recvs(N), net.recvs()
+    s_h, s_h2 = net.sends(g4.at[c, pl.ds(0, 63)]), net.sends(g4.at[c])
+    for kz, ky in FAR:
+        pool = net.chip((z + kz) % N, (y + ky) % N, c)
+        net.put(g4.at[c, me], g4.at[c, me], s_h, r_h + z, pool)
+    gain = gain_ref[...].astype(F32)
+    wg = jnp.concatenate([gate_ref[...].astype(F32), up_ref[...].astype(F32)], 0)
+    wg = (wg * gain).astype(BF16)
+    for g in range(8):
+        feat = const_ref[2:3, 128 * g : 128 * g + 128]
+        spot = (iota((DEV, 128), 0).astype(F32) == feat).astype(F32).astype(BF16)
+        place[:, 128 * g : 128 * g + 128] = spot
+        wgp[:, 128 * g : 128 * g + 128] = nn(wg, spot).astype(BF16)
+    for k in (0, 1, 7, 2, 6, 3, 5, 4):
+        t = (z + k) % N
+        net.got(g4.at[c, pl.ds(0, 8 if k else 7)], r_h + t)
+        line = g4.at[c, pl.ds(t * N, N)]
+        net.put(line, line, s_h2, r_h2, net.sib)
+    net.got(g4.at[1 - c], r_h2)
+
+    for d in (0, 1):
+        resid = g4[d].reshape(1024, 128)
+        gu_buf[x, :, 128 * d : 128 * d + 128] = nn(wgp[...], resid).astype(BF16)
         wide = resid.astype(F32)
         square = jnp.sum(wide * wide, 0, keepdims=True)
         sq_buf[x, :, 128 * d : 128 * d + 128] = jnp.broadcast_to(square, (8, 128))
@@ -447,13 +453,8 @@
     for d in (0, 1):
         pick = iota((8, 128), 1) + 128 * d == 2 * p + iota((8, 128), 0)
         pick = jnp.logical_and(pick, iota((8, 128), 0) < 2)
-        mine = nt(pick.astype(F32).astype(BF16), gh[d].reshape(DEV, 128)).astype(BF16)
-        feat = const_ref[2 + d : 3 + d, :DEV]
-        parts = []
-        for g in range(6):
-            place = iota((128, DEV), 0).astype(F32) + 128.0 * g == feat
-            parts.append(nt(mine, place.astype(F32).astype(BF16)))
-        own_resid = own_resid + jnp.concatenate(parts, 1)
+        mine = nt(pick.astype(F32).astype(BF16), g4[d].reshape(1024, 128)).astype(BF16)
+        own_resid = own_resid + nt(mine, place[...])
     net.got(gu_buf.at[pl.ds(0, 3)], r_gu)
     net.got(sq_buf.at[pl.ds(0, 3)], r_sq)
     gu = gu_buf[0].astype(F32)
@@ -468,49 +469,44 @@
     hidden_t = hidden.T.astype(BF16)
 
     down = down_ref[...]
-    rows = [nn(to_order0, hidden_t).astype(BF16), hidden_t]
-    for d in (0, 1):
-        part = nn(rows[d], down[:, HALF * d : HALF * d + HALF]).astype(BF16)
-        for s in range(N):
-            dbuf[d, s] = part[32 * s : 32 * s + 32]
-    r_d = net.recvs()
-    net.spread(dbuf, d_slot, r_d, along_first=False, pick=True)
-    net.spread_wait(d_slot, r_d)
-    part = d_slot[0].astype(F32)
-    for j in range(1, 16):
-        part = part + d_slot[j].astype(F32)
-    for f in range(N):
-        for e in (0, 1):
-            b_src[f, e] = part[4 * f + 2 * e : 4 * f + 2 * e + 2]
-    r_b = net.recvs()
-    s_b = net.sends(b_slot.at[pl.ds(0, 15)])
-    own = c * N + fi
-    for k in (4, 3, 5, 2, 6, 1, 7):
-        t = (fi + k) % N
-        for e in (0, 1):
-            pool = net.chip(t * (1 - c) + z * c, y * (1 - c) + t * c, e)
-            net.put(b_src.at[t, e], b_slot.at[own], s_b, r_b, pool)
-    net.put(b_src.at[fi, 1 - c], b_slot.at[own], s_b, r_b, net.sib)
-    b_slot[own] = b_src[fi, c]
-    net.got(b_slot.at[pl.ds(0, 15)], r_b)
-    for d in (0, 1):
-        total = b_slot[N * d]
-        for f in range(1, N):
-            total = total + b_slot[N * d + f]
-        out_ref[:, HALF * d : HALF * d + HALF] = (
-            own_resid[0:2, HALF * d : HALF * d + HALF] + total
-        ).astype(BF16)
+    rows = nn(to_core, hidden_t).astype(BF16)
+    for e in (0, 1):
+        part = nn(rows[128 * e : 128 * e + 128], down).astype(BF16)
+        dbuf[e] = part.reshape(N, 16, DEV)
+    r_d, r_b = net.recvs(N), net.recvs()
+    s_d, s_b = net.sends(dbuf.at[0]), net.sends(b_slot.at[pl.ds(0, 63)])
+    order = (4, 3, 5, 2, 6, 1, 7, 0)
+    for k in order:
+        t = (z + k) % N
+        net.put(dbuf.at[1 - c, t], d_slot.at[t], s_d, r_d + t, net.sib)
+    for k in order:
+        t = (z + k) % N
+        net.got(d_slot.at[t], r_d + t)
+        part = dbuf[c, t].astype(F32) + d_slot[t].astype(F32)
+        for j in range(N):
+            b_src[t, j] = part[2 * j : 2 * j + 2].astype(BF16)
+        for ky in order:
+            if k or ky:
+                v = (y + ky) % N
+                net.put(b_src.at[t, v], b_slot.at[me], s_b, r_b, net.chip(t, v, c))
+    b_slot[me] = b_src[z, y]
+    net.got(b_slot.at[pl.ds(0, 63)], r_b)
+    sums = [b_slot[j].astype(F32) for j in range(4)]
+    for j in range(4, 64):
+        sums[j % 4] = sums[j % 4] + b_slot[j].astype(F32)
+    total = (sums[0] + sums[1]) + (sums[2] + sums[3])
+    out_ref[...] = (own_resid[0:2] + total).astype(BF16)
 
     net.finish()
     for k in range(X):
 
-        @pl.when(jnp.logical_not(jnp.logical_and(home, x == k)))
+        @pl.when(jnp.logical_not(jnp.logical_and(home, kept == k)))
         def _(k=k):
             copies[k].wait_send()
 
 
 SENDS = 32
-RECVS = 72
+RECVS = 80
 
 
 def scratch():
@@ -525,12 +521,11 @@
         v((2, N, 32, 512), BF16), v((2, N, 32, HALF), BF16), v((2, N, 32, HALF), BF16),
         v((2, 8, HALF), BF16), v((2, 8, 128), F32), v((16, 8, HALF), BF16), v((16, 8, 128), F32),
         v((80, HALF), F32), v((2, N, 128, HALF), BF16), v((2, N, 8, 128), F32),
-        v((2, REQ, 1024), F32), v((4, REQ, 1024), BF16), v((2, REQ, HALF), BF16),
-        v((2, 128, DEV), BF16),
-        v((X, 6, REQ), F32), v((X, 6, REQ), F32),
-        v((2, 6, 128), F32), v((16, 6, 128), F32), v((96, 128), F32), v((2, N, 96, 128), BF16),
+        v((2, REQ, 1024), F32), v((8, REQ, 1024), BF16), v((2, REQ, HALF), BF16),
+        v((128, 1024), BF16), v((DEV, 1024), BF16),
+        v((X, 12, 128), F32), v((X, 12, 128), F32), v((2, 64, 16, 128), BF16),
         v((X, 128, REQ), BF16), v((X, 8, REQ), F32),
-        v((2, N, 32, HALF), BF16), v((16, 32, HALF), BF16), v((N, 2, 2, HALF), F32), v((16, 2, HALF), F32),
+        v((2, N, 16, DEV), BF16), v((N, 16, DEV), BF16), v((N, N, 2, DEV), BF16), v((64, 2, DEV), BF16),
         pltpu.SemaphoreType.DMA((SENDS,)), pltpu.SemaphoreType.DMA((RECVS,)),
         pltpu.SemaphoreType.DMA((14,)),
     ]

time: 87.4 us -> 84.2 us (0.963)
  Pallas kernels: 84.7 us -> 81.5 us
    pallas_call x1, Pallas kernels: 84.7 us -> 81.5 us  [per_device(): pl.pallas_call(kernel, out_shape=jax.ShapeDtypeStruct((2, DEV), BF16), in...]
where the time goes in v3:
time: 84.2 us; the launch traced here: 84 us
  Pallas kernels  81.5 us (97%)
  local copies, waits for them, and re-layouts  2.53 us (3%)
    pallas_call x1, Pallas kernels, per_device(): pl.pallas_call(kernel, out_shape=jax.ShapeDtypeStruct((2, DEV), BF16), in...  81.5 us

profile of v3, /device:TPU:1, one launch (start us, length us, event | category | flops | bytes accessed | tf_op | source)
XLA Modules:
  0.0 84.0 jit_solution(15359481731325186842)
XLA Ops:
  0.0 1.3 %reshape.3.gain_hbm = bf16[1,768]{1,0:T(2,128)(2,1)} reshape(bf16[768]{0:T(1024)(128)(2,1)} %param.23) | data formatting | bytes 3072 | tf_op jit(solution)/shard_map/reshape | solution.py:552
  1.3 81.5 %layer.1 = bf16[2,768]{1,0:T(2,128)(2,1)} custom-call(bf16[2,768]{1,0:T(2,128)(2,1)} %q_hbm.1, bf16[2,768]{1,0:T(2,128)(2,1)} %k_hbm.1, bf16[2,768]{1,0:T(2,128)(2,1)} %v_hbm.1, bf16[2,768]{1,0:T(2,128)(2,1)} %res_hbm.1, s32[2,8]{1,0:T(2,128)} %tab_hbm.1, s32[2]{0:T(128)} %len_hbm.1, f32[8,1024]{1,0:T(8,128)} %constant.2.clone.const_hbm, ...), custom_call_target="tpu_custom_call" | custom-call | tf_op jit(solution)/shard_map/layer/pallas_call | solution.py:540
  82.8 1.3 %copy.16 = bf16[2,768]{1,0:T(2,128)(2,1)} copy(bf16[2,768]{1,0:T(2,128)(2,1)} %layer.1) | data formatting | bytes 6144

commit v4 on v3

--- a/solution.py
+++ b/solution.py
@@ -160,7 +160,7 @@
     down_ref, kbuf, vbuf,
     pay, vr, slot1, slot2, line1, line2, g1, gv, gr,
     acc_src, lse_src, acc_slot, lse_slot, acc_line, ga, gl,
-    bias, ebuf, attb, wgp, place, s3_src, s3_slot, g4,
+    bias, ebuf, attb, wgain, wgp, place, s3_src, s3_slot, g4,
     gu_buf, sq_buf, dbuf, d_slot, b_src, b_slot,
     send, recv, local,
 ):
@@ -185,8 +185,8 @@
 
     for k in range(1, N):
         for e in (0, 1):
-            hello(net.chip((z + k) % N, y, e), x)
-            hello(net.chip(z, (y + k) % N, e), x)
+            hello(net.chip(z + (1 - c) * ((z + k) % N - z), y + c * ((y + k) % N - y), e), x)
+        hello(net.chip(z + c * ((z + k) % N - z), y + (1 - c) * ((y + k) % N - y), c), x)
     hello(net.sib, x)
     for k in range(1, X):
         hello(p, (x + k) % X)
@@ -239,7 +239,7 @@
         vr[d, :, :HALF] = v_ref[:, HALF * d : HALF * d + HALF]
         vr[d, :, HALF:] = res_ref[:, HALF * d : HALF * d + HALF]
 
-    pl.semaphore_wait(barrier, 36 - jnp.where(home, 1, 0))
+    pl.semaphore_wait(barrier, 29 - jnp.where(home, 1, 0))
 
     r_pay, r_vr = net.recvs(), net.recvs()
     net.spread(pay, slot1, r_pay)
@@ -254,6 +254,20 @@
     to_core = (nat_row == n_col).astype(F32).astype(BF16)
     to_natural = (o_row == nat_col).astype(F32).astype(BF16)
 
+    for load in loads[7:10]:
+        load.wait()
+    gain = gain_ref[...].astype(F32)
+    wg = jnp.concatenate([gate_ref[...].astype(F32), up_ref[...].astype(F32)], 0)
+    wgain[...] = (wg * gain).astype(BF16)
+
+    def prepare(groups):
+        for g in groups:
+            feat = const_ref[2:3, 128 * g : 128 * g + 128]
+            spot = (iota((DEV, 128), 0).astype(F32) == feat).astype(F32).astype(BF16)
+            place[:, 128 * g : 128 * g + 128] = spot
+            wgp[:, 128 * g : 128 * g + 128] = nn(wgain[...], spot).astype(BF16)
+
+    prepare(range(4))
     net.spread_wait(slot1, r_pay)
     for j in range(16):
         line1[2 * j : 2 * j + 2, :] = slot1[j].astype(F32)
@@ -291,7 +305,7 @@
     sub = iota((8, DEV), 0)
     head_mask = jnp.logical_and(lane >= 96 * sub, lane < 96 * sub + 96)
     query = jnp.concatenate(queries, 1)
-    for load in loads[7:]:
+    for load in loads[10:]:
         load.wait()
     acc = jnp.zeros((8, DEV), F32)
     tiles = [jnp.zeros((8, 128), F32), jnp.zeros((8, 128), F32)]
@@ -397,6 +411,7 @@
         s3_slot[x] = s3_src[kept]
 
     net.line_forward(r_line)
+    prepare(range(4, 8))
     net.line_wait(r_line)
     feature = 384 * (z % 2) + 48 * y + 24 * (group % 2) + 12 * (z // 4) + iota((16, HALF), 0)
     inputs = []
@@ -423,14 +438,6 @@
     for kz, ky in FAR:
         pool = net.chip((z + kz) % N, (y + ky) % N, c)
         net.put(g4.at[c, me], g4.at[c, me], s_h, r_h + z, pool)
-    gain = gain_ref[...].astype(F32)
-    wg = jnp.concatenate([gate_ref[...].astype(F32), up_ref[...].astype(F32)], 0)
-    wg = (wg * gain).astype(BF16)
-    for g in range(8):
-        feat = const_ref[2:3, 128 * g : 128 * g + 128]
-        spot = (iota((DEV, 128), 0).astype(F32) == feat).astype(F32).astype(BF16)
-        place[:, 128 * g : 128 * g + 128] = spot
-        wgp[:, 128 * g : 128 * g + 128] = nn(wg, spot).astype(BF16)
     for k in (0, 1, 7, 2, 6, 3, 5, 4):
         t = (z + k) % N
         net.got(g4.at[c, pl.ds(0, 8 if k else 7)], r_h + t)
@@ -438,30 +445,27 @@
         net.put(line, line, s_h2, r_h2, net.sib)
     net.got(g4.at[1 - c], r_h2)
 
+    r_gu, r_sq = net.recvs(), net.recvs()
+    s_gu, s_sq = net.sends(gu_buf.at[pl.ds(0, 3)]), net.sends(sq_buf.at[pl.ds(0, 3)])
     for d in (0, 1):
         resid = g4[d].reshape(1024, 128)
-        gu_buf[x, :, 128 * d : 128 * d + 128] = nn(wgp[...], resid).astype(BF16)
-        wide = resid.astype(F32)
+        gu_buf[x, d] = nn(wgp[...], resid).astype(BF16)
+        for k in (2, 1, 3):
+            net.put(gu_buf.at[x, d], gu_buf.at[x, d], s_gu, r_gu, p, (x + k) % X)
+    for d in (0, 1):
+        wide = g4[d].reshape(1024, 128).astype(F32)
         square = jnp.sum(wide * wide, 0, keepdims=True)
         sq_buf[x, :, 128 * d : 128 * d + 128] = jnp.broadcast_to(square, (8, 128))
-    r_gu, r_sq = net.recvs(), net.recvs()
-    s_gu, s_sq = net.sends(gu_buf.at[pl.ds(0, 3)]), net.sends(sq_buf.at[pl.ds(0, 3)])
     for k in (2, 1, 3):
-        net.put(gu_buf.at[x], gu_buf.at[x], s_gu, r_gu, p, (x + k) % X)
         net.put(sq_buf.at[x], sq_buf.at[x], s_sq, r_sq, p, (x + k) % X)
-    own_resid = jnp.zeros((8, DEV), F32)
-    for d in (0, 1):
-        pick = iota((8, 128), 1) + 128 * d == 2 * p + iota((8, 128), 0)
-        pick = jnp.logical_and(pick, iota((8, 128), 0) < 2)
-        mine = nt(pick.astype(F32).astype(BF16), g4[d].reshape(1024, 128)).astype(BF16)
-        own_resid = own_resid + nt(mine, place[...])
     net.got(gu_buf.at[pl.ds(0, 3)], r_gu)
     net.got(sq_buf.at[pl.ds(0, 3)], r_sq)
-    gu = gu_buf[0].astype(F32)
+    sums = [gu_buf[0, d].astype(F32) for d in (0, 1)]
     square = sq_buf[0]
     for k in range(1, X):
-        gu = gu + gu_buf[k].astype(F32)
+        sums = [sums[d] + gu_buf[k, d].astype(F32) for d in (0, 1)]
         square = square + sq_buf[k]
+    gu = jnp.concatenate(sums, 1)
     inv = lax.rsqrt(square[0:1] * (1.0 / (X * DEV)) + 1e-05)
     gate = gu[:FFD] * inv
     up = gu[FFD:] * inv
@@ -490,6 +494,12 @@
                 v = (y + ky) % N
                 net.put(b_src.at[t, v], b_slot.at[me], s_b, r_b, net.chip(t, v, c))
     b_slot[me] = b_src[z, y]
+    mine = jnp.zeros((8, 1024), F32)
+    for d in (0, 1):
+        pick = iota((8, 128), 1) + 128 * d == 2 * p + iota((8, 128), 0)
+        pick = jnp.logical_and(pick, iota((8, 128), 0) < 2)
+        mine = mine + nt(pick.astype(F32).astype(BF16), g4[d].reshape(1024, 128))
+    own_resid = nt(mine.astype(BF16), place[...])
     net.got(b_slot.at[pl.ds(0, 63)], r_b)
     sums = [b_slot[j].astype(F32) for j in range(4)]
     for j in range(4, 64):
@@ -522,9 +532,9 @@
         v((2, 8, HALF), BF16), v((2, 8, 128), F32), v((16, 8, HALF), BF16), v((16, 8, 128), F32),
         v((80, HALF), F32), v((2, N, 128, HALF), BF16), v((2, N, 8, 128), F32),
         v((2, REQ, 1024), F32), v((8, REQ, 1024), BF16), v((2, REQ, HALF), BF16),
-        v((128, 1024), BF16), v((DEV, 1024), BF16),
+        v((128, DEV), BF16), v((128, 1024), BF16), v((DEV, 1024), BF16),
         v((X, 12, 128), F32), v((X, 12, 128), F32), v((2, 64, 16, 128), BF16),
-        v((X, 128, REQ), BF16), v((X, 8, REQ), F32),
+        v((X, 2, 128, 128), BF16), v((X, 8, REQ), F32),
         v((2, N, 16, DEV), BF16), v((N, 16, DEV), BF16), v((N, N, 2, DEV), BF16), v((64, 2, DEV), BF16),
         pltpu.SemaphoreType.DMA((SENDS,)), pltpu.SemaphoreType.DMA((RECVS,)),
         pltpu.SemaphoreType.DMA((14,)),

time: 84.2 us -> 83.5 us (level)
  no operation moved by 1% of the time
where the time goes in v4:
time: 83.5 us; the launch traced here: 83.3 us
  Pallas kernels  80.8 us (97%)
  local copies, waits for them, and re-layouts  2.53 us (3%)
    pallas_call x1, Pallas kernels, per_device(): pl.pallas_call(kernel, out_shape=jax.ShapeDtypeStruct((2, DEV), BF16), in...  80.8 us

profile of v4, /device:TPU:1, one launch (start us, length us, event | category | flops | bytes accessed | tf_op | source)
XLA Modules:
  0.0 83.3 jit_solution(1037121941209771307)
XLA Ops:
  0.0 1.3 %reshape.3.gain_hbm = bf16[1,768]{1,0:T(2,128)(2,1)} reshape(bf16[768]{0:T(1024)(128)(2,1)} %param.23) | data formatting | bytes 3072 | tf_op jit(solution)/shard_map/reshape | solution.py:562
  1.3 80.8 %layer.1 = bf16[2,768]{1,0:T(2,128)(2,1)} custom-call(bf16[2,768]{1,0:T(2,128)(2,1)} %q_hbm.1, bf16[2,768]{1,0:T(2,128)(2,1)} %k_hbm.1, bf16[2,768]{1,0:T(2,128)(2,1)} %v_hbm.1, bf16[2,768]{1,0:T(2,128)(2,1)} %res_hbm.1, s32[2,8]{1,0:T(2,128)} %tab_hbm.1, s32[2]{0:T(128)} %len_hbm.1, f32[8,1024]{1,0:T(8,128)} %constant.2.clone.const_hbm, ...), custom_call_target="tpu_custom_call" | custom-call | tf_op jit(solution)/shard_map/layer/pallas_call | solution.py:550
  82.1 1.3 %copy.16 = bf16[2,768]{1,0:T(2,128)(2,1)} copy(bf16[2,768]{1,0:T(2,128)(2,1)} %layer.1) | data formatting | bytes 6144
